TPU v7x, 32 devices: a whole 2x2x4 slice. The times are simulated.
32 devices in a mesh: dp: 8 (over z, x), segment: 4 (over y, core).
Axes of the slice: x: 2, y: 2, z: 4, core: 2. Of those that a mesh axis runs over, the one named last changes fastest.
Arguments:
- features: bfloat16 [1536, 640], P('dp'), may hold values from -6 to 6
- timesteps: int32 [24], P('dp'), may hold values from 0 to 999
- text_ids: int32 [24, 64], replicated, may hold values from 0 to 16383
- text_table: bfloat16 [16384, 640], P(('dp', 'segment')), may hold values from -12 to 12
- in_weights: bfloat16 [4, 640, 640], P('segment'), may hold values from -0.25 to 0.25
- out_weights: bfloat16 [4, 640, 640], P('segment'), may hold values from -0.25 to 0.25
- skip_weights: bfloat16 [4, 640, 640], P('segment'), may hold values from -0.25 to 0.25
- cotangent: bfloat16 [1536, 640], P('dp'), may hold values from -0.15234375 to 0.15234375
Outputs:
- in_grads: float32 [4, 640, 640], P('segment', 'dp')
- out_grads: float32 [4, 640, 640], P('segment', 'dp')
- skip_grads: float32 [4, 640, 640], P('segment', 'dp')
All inputs are finite; a program needn't handle non-finite values.
Results may differ from a plain program's by a relative error of at most 0.033.
Values may be sent and summed in bfloat16 or wider, within the bound.
No kernel may reach another device: no remote copies, remote signals or barrier semaphores. Data moves between devices by JAX's collectives and lax.ppermute only.
A program may use at most 64 MiB of HBM per device.

v0:
```python
import math

import jax
import jax.numpy as jnp
from jax import lax
from jax.sharding import PartitionSpec as P

GROUPS = 32


EPSILON = 1e-05


def shifted_2(value, axis, steps):
    count = lax.axis_size(axis)
    initial, last = (max(0, -steps), min(count, count - steps))
    return lax.ppermute(value, axis, [(source, source + steps) for source in range(initial, last)])


def partner(block, axis, bit):
    count = lax.axis_size(axis)
    route = []
    for low in range(count):
        high = low | 1 << bit
        if high != low and high < count:
            route += [(low, high), (high, low)]
    return lax.ppermute(block, axis, route)


def grouped(vector):
    lead = vector.shape[:-1]
    split = vector.reshape(lead + (GROUPS, vector.shape[-1] // GROUPS))
    total = jnp.sum(split, axis=-1, keepdims=True)
    return jnp.broadcast_to(total, split.shape).reshape(vector.shape)


def normalize(block):
    group_size = block.shape[-2] * (block.shape[-1] // GROUPS)
    center = grouped(jnp.sum(block, axis=-2, keepdims=True)) / group_size
    shifted = block - center
    spread = grouped(jnp.sum(shifted * shifted, axis=-2, keepdims=True)) / group_size
    inv_scale = lax.rsqrt(spread + EPSILON)
    return (shifted * inv_scale, inv_scale)


def normalize_back(d_normed, normed, inv_scale):
    group_size = normed.shape[-2] * (normed.shape[-1] // GROUPS)
    mean_first = grouped(jnp.sum(d_normed, axis=-2, keepdims=True)) / group_size
    mean_second = grouped(jnp.sum(d_normed * normed, axis=-2, keepdims=True)) / group_size
    return inv_scale * (d_normed - mean_first - normed * mean_second)


def matmul(left, weight):
    in_shape = left.shape
    flattened = left.reshape(-1, in_shape[-1])
    product = jnp.dot(flattened, weight, preferred_element_type=jnp.float32)
    return product.reshape(in_shape[:-1] + (weight.shape[1],))


def matmul_transposed(left, weight):
    in_shape = left.shape
    flattened = left.reshape(-1, in_shape[-1])
    product = lax.dot_general(
        flattened, weight, (((1,), (1,)), ((), ())), preferred_element_type=jnp.float32
    )
    return product.reshape(in_shape[:-1] + (weight.shape[0],))


def swish_slope(pre_act):
    sigmoid_val = jax.nn.sigmoid(pre_act)
    return sigmoid_val * (1.0 + pre_act * (1.0 - sigmoid_val))


def encode_core(state_in, weight_in, weight_out, condition):
    current = state_in.astype(jnp.float32)
    normed, inv_scale = normalize(current)
    normed_low = normed.astype(jnp.bfloat16)
    pre_act = matmul(normed_low, weight_in) + condition
    hidden = jax.nn.silu(pre_act).astype(jnp.bfloat16)
    result = (current + matmul(hidden, weight_out)).astype(jnp.bfloat16)
    return (current, normed, inv_scale, normed_low, pre_act, hidden, result)


def encode(state_in, weight_in, weight_out, weight_skip, condition):
    parts = encode_core(state_in, weight_in, weight_out, condition)
    result = parts[6]
    skip_out = matmul(result, weight_skip).astype(jnp.bfloat16)
    return (result, skip_out)


def encode_back(
    state_in, weight_in, weight_out, weight_skip, condition, d_result, d_skip, weight_grad
):
    current, normed, inv_scale, normed_low, pre_act, hidden, result = encode_core(
        state_in, weight_in, weight_out, condition
    )
    d_total = d_result.astype(jnp.float32) + matmul_transposed(d_skip, weight_skip)
    grad_skip = weight_grad(result, d_skip)
    d_total_low = d_total.astype(jnp.bfloat16)
    grad_out = weight_grad(hidden, d_total_low)
    d_act = (matmul_transposed(d_total_low, weight_out) * swish_slope(pre_act)).astype(jnp.bfloat16)
    grad_in = weight_grad(normed_low, d_act)
    d_normed = matmul_transposed(d_act, weight_in)
    d_inputs = (d_total + normalize_back(d_normed, normed, inv_scale)).astype(jnp.bfloat16)
    return (d_inputs, grad_in, grad_out, grad_skip)


def decode_core(state_in, skip_in, weight_in, weight_skip, condition):
    current = state_in.astype(jnp.float32) + matmul(skip_in, weight_skip)
    normed, inv_scale = normalize(current)
    normed_low = normed.astype(jnp.bfloat16)
    pre_act = matmul(normed_low, weight_in) + condition
    hidden = jax.nn.silu(pre_act).astype(jnp.bfloat16)
    return (current, normed, inv_scale, normed_low, pre_act, hidden)


def decode(state_in, skip_in, weight_in, weight_out, weight_skip, condition):
    current, normed, inv_scale, normed_low, pre_act, hidden = decode_core(
        state_in, skip_in, weight_in, weight_skip, condition
    )
    return (current + matmul(hidden, weight_out)).astype(jnp.bfloat16)


def decode_back(
    state_in, skip_in, weight_in, weight_out, weight_skip, condition, d_result, weight_grad
):
    current, normed, inv_scale, normed_low, pre_act, hidden = decode_core(
        state_in, skip_in, weight_in, weight_skip, condition
    )
    grad_out = weight_grad(hidden, d_result)
    d_act = (matmul_transposed(d_result, weight_out) * swish_slope(pre_act)).astype(jnp.bfloat16)
    grad_in = weight_grad(normed_low, d_act)
    d_normed = matmul_transposed(d_act, weight_in)
    d_current = (d_result.astype(jnp.float32) + normalize_back(d_normed, normed, inv_scale)).astype(
        jnp.bfloat16
    )
    grad_skip = weight_grad(skip_in, d_current)
    d_skip = matmul_transposed(d_current, weight_skip).astype(jnp.bfloat16)
    return (d_current, d_skip, grad_in, grad_out, grad_skip)


def time_embedding(steps, channels):
    half_width = channels // 2
    freqs = jnp.exp(-math.log(10000.0) * jnp.arange(half_width, dtype=jnp.float32) / half_width)
    angles = steps.astype(jnp.float32)[:, None] * freqs[None, :]
    return jnp.concatenate([jnp.cos(angles), jnp.sin(angles)], axis=-1)


def local_grad(left, right):
    left_flat = left.reshape(-1, left.shape[-1])
    right_flat = right.reshape(-1, right.shape[-1])
    return lax.dot_general(
        left_flat, right_flat, (((0,), (0,)), ((), ())), preferred_element_type=jnp.float32
    )


def take_slot(buffer, chosen_slot):
    return lax.dynamic_slice_in_dim(buffer, chosen_slot, 1, 0)


def store_slot(buffer, chosen_slot, update, active):
    existing = take_slot(buffer, chosen_slot)
    return lax.dynamic_update_slice_in_dim(
        buffer, jnp.where(active, update, existing), chosen_slot, 0
    )


def pass_up(block):
    return shifted_2(block, "segment", 1)


def pass_down(block):
    return shifted_2(block, "segment", -1)


def mirror(buffer):
    bit_count = lax.axis_size("segment").bit_length() - 1
    bit_order = list(range(bit_count))
    for bit_number in bit_order:
        buffer = partner(buffer, "segment", bit_number)
    return buffer


def on_device(
    features, timesteps, text_ids, text_table, in_weights, out_weights, skip_weights, cotangent
):
    segments = lax.axis_size("segment")
    half_segments = segments // 2
    segment_index = lax.axis_index("segment")
    channels = features.shape[-1]
    micro_count = timesteps.shape[0]
    row_count = features.shape[0] // micro_count
    samples = features.reshape(micro_count, row_count, channels)
    cot_blocks = cotangent.reshape(micro_count, row_count, channels)
    weight_in = in_weights[0]
    weight_out = out_weights[0]
    weight_skip = skip_weights[0]
    vocab_rows = text_table.shape[0]
    first_word = lax.axis_index(("dp", "segment")) * vocab_rows
    vocab_ids = first_word + lax.iota(jnp.int32, vocab_rows)
    counts = jnp.sum(
        (text_ids[None, :, :] == vocab_ids[:, None, None]).astype(jnp.float32), axis=-1
    )
    partial_sum = (
        lax.dot_general(
            counts.astype(jnp.bfloat16),
            text_table,
            (((0,), (0,)), ((), ())),
            preferred_element_type=jnp.float32,
        )
        / text_ids.shape[1]
    )
    pooled_all = lax.psum(partial_sum, ("dp", "segment"))
    dp_index = lax.axis_index("dp")
    pooled = lax.dynamic_slice_in_dim(pooled_all, dp_index * micro_count, micro_count, 0)
    condition = time_embedding(timesteps, channels) + pooled

    def cond_at(chosen_slot):
        return lax.dynamic_slice_in_dim(condition, chosen_slot, 1, 0)[:, None, :]

    zero_block = jnp.zeros((1, row_count, channels), jnp.bfloat16)
    zero_matrix = jnp.zeros((channels, channels), jnp.float32)
    zero_buffer = jnp.zeros((micro_count, row_count, channels), jnp.bfloat16)

    def slot_of(micro_index):
        return jnp.clip(micro_index, 0, micro_count - 1).astype(jnp.int32)

    def enc_step(moment, loop_state):
        incoming, inputs_buf, skips_buf, bottom_buf = loop_state
        micro_index = moment - segment_index
        active = (segment_index < half_segments) & (micro_index >= 0) & (micro_index < micro_count)
        chosen_slot = slot_of(micro_index)
        entering = jnp.where(segment_index == 0, take_slot(samples, chosen_slot), incoming)
        result, skip_out = lax.cond(
            active,
            lambda: encode(entering, weight_in, weight_out, weight_skip, cond_at(chosen_slot)),
            lambda: (zero_block, zero_block),
        )
        inputs_buf = store_slot(inputs_buf, chosen_slot, entering, active)
        skips_buf = store_slot(skips_buf, chosen_slot, skip_out, active)
        arrived = pass_up(result)
        landed = moment - (half_segments - 1)
        land_ok = (segment_index == half_segments) & (landed >= 0) & (landed < micro_count)
        bottom_buf = store_slot(bottom_buf, slot_of(landed), arrived, land_ok)
        return (arrived, inputs_buf, skips_buf, bottom_buf)

    incoming, inputs_buf, skips_buf, bottom_buf = lax.fori_loop(
        0,
        half_segments + micro_count - 1,
        enc_step,
        (zero_block, zero_buffer, zero_buffer, zero_buffer),
    )
    mirrored = mirror(skips_buf)

    def dec_step(moment, loop_state):
        incoming, inputs_buf = loop_state
        micro_index = moment - (segment_index - half_segments)
        active = (segment_index >= half_segments) & (micro_index >= 0) & (micro_index < micro_count)
        chosen_slot = slot_of(micro_index)
        entering = jnp.where(
            segment_index == half_segments, take_slot(bottom_buf, chosen_slot), incoming
        )
        result = lax.cond(
            active,
            lambda: decode(
                entering,
                take_slot(mirrored, chosen_slot),
                weight_in,
                weight_out,
                weight_skip,
                cond_at(chosen_slot),
            ),
            lambda: zero_block,
        )
        inputs_buf = store_slot(inputs_buf, chosen_slot, entering, active)
        return (pass_up(result), inputs_buf)

    incoming, inputs_buf = lax.fori_loop(
        0, half_segments + micro_count - 2, dec_step, (zero_block, inputs_buf)
    )
    inputs_buf = store_slot(inputs_buf, micro_count - 1, incoming, segment_index == segments - 1)

    def dec_back_step(moment, loop_state):
        incoming, grad_sums, dskip_buf, top_buf = loop_state
        micro_index = moment - (segments - 1 - segment_index)
        active = (segment_index >= half_segments) & (micro_index >= 0) & (micro_index < micro_count)
        chosen_slot = slot_of(micro_index)
        entering = jnp.where(
            segment_index == segments - 1, take_slot(cot_blocks, chosen_slot), incoming
        )

        def dec_run_branch():
            d_current, d_skip, grad_in, grad_out, grad_skip = decode_back(
                take_slot(inputs_buf, chosen_slot),
                take_slot(mirrored, chosen_slot),
                weight_in,
                weight_out,
                weight_skip,
                cond_at(chosen_slot),
                entering,
                local_grad,
            )
            return (d_current, d_skip, (grad_in, grad_out, grad_skip))

        def dec_spare_branch():
            return (zero_block, zero_block, (zero_matrix, zero_matrix, zero_matrix))

        d_current, d_skip, new_grads = lax.cond(active, dec_run_branch, dec_spare_branch)
        grad_sums = tuple((old + new for old, new in zip(grad_sums, new_grads)))
        dskip_buf = store_slot(dskip_buf, chosen_slot, d_skip, active)
        arrived = pass_down(d_current)
        landed = moment - (half_segments - 1)
        land_ok = (segment_index == half_segments - 1) & (landed >= 0) & (landed < micro_count)
        top_buf = store_slot(top_buf, slot_of(landed), arrived, land_ok)
        return (arrived, grad_sums, dskip_buf, top_buf)

    zero_grads = (zero_matrix, zero_matrix, zero_matrix)
    incoming, grad_sums, dskip_buf, top_buf = lax.fori_loop(
        0,
        half_segments + micro_count - 1,
        dec_back_step,
        (zero_block, zero_grads, zero_buffer, zero_buffer),
    )
    skip_grads_in = mirror(dskip_buf)

    def enc_back_compute(moment, incoming, grad_sums):
        micro_index = moment - (half_segments - 1 - segment_index)
        active = (segment_index < half_segments) & (micro_index >= 0) & (micro_index < micro_count)
        chosen_slot = slot_of(micro_index)
        entering = jnp.where(
            segment_index == half_segments - 1, take_slot(top_buf, chosen_slot), incoming
        )

        def enc_run_branch():
            d_inputs, grad_in, grad_out, grad_skip = encode_back(
                take_slot(inputs_buf, chosen_slot),
                weight_in,
                weight_out,
                weight_skip,
                cond_at(chosen_slot),
                entering,
                take_slot(skip_grads_in, chosen_slot),
                local_grad,
            )
            return (d_inputs, (grad_in, grad_out, grad_skip))

        def enc_spare_branch():
            return (zero_block, (zero_matrix, zero_matrix, zero_matrix))

        d_inputs, new_grads = lax.cond(active, enc_run_branch, enc_spare_branch)
        grad_sums = tuple((old + new for old, new in zip(grad_sums, new_grads)))
        return (d_inputs, grad_sums)

    def enc_back_step(moment, loop_state):
        incoming, grad_sums = loop_state
        d_inputs, grad_sums = enc_back_compute(moment, incoming, grad_sums)
        return (pass_down(d_inputs), grad_sums)

    last_moment = half_segments + micro_count - 2
    incoming, grad_sums = lax.fori_loop(0, last_moment, enc_back_step, (zero_block, grad_sums))
    unused_inputs, grad_sums = enc_back_compute(last_moment, incoming, grad_sums)
    grad_in, grad_out, grad_skip = (
        lax.psum_scatter(
            grad_sums[0].astype(jnp.bfloat16), "dp", scatter_dimension=0, tiled=True
        ).astype(jnp.float32),
        lax.psum_scatter(
            grad_sums[1].astype(jnp.bfloat16), "dp", scatter_dimension=0, tiled=True
        ).astype(jnp.float32),
        lax.psum_scatter(
            grad_sums[2].astype(jnp.bfloat16), "dp", scatter_dimension=0, tiled=True
        ).astype(jnp.float32),
    )
    return (grad_in[None], grad_out[None], grad_skip[None])


def solution(mesh):
    in_specs = (
        P("dp", None),
        P("dp"),
        P(),
        P(("dp", "segment"), None),
        P("segment", None, None),
        P("segment", None, None),
        P("segment", None, None),
        P("dp", None),
    )
    out_specs = (P("segment", "dp", None), P("segment", "dp", None), P("segment", "dp", None))
    return jax.shard_map(
        on_device, mesh=mesh, in_specs=in_specs, out_specs=out_specs, check_vma=False
    )
```

profile of v0, /device:TPU:0, one launch (start us, length us, event | category | flops | bytes accessed | tf_op | source)
XLA Modules:
  0.0 515.0 jit_solution(3807118447064778023)
XLA Ops:
  8.9 42.6 %psum.7 = f32[24,640]{1,0:T(8,128)S(1)} all-reduce(f32[24,640]{1,0:T(8,128)S(1)} %convolution_multiply_fusion.3), channel_id=1, replica_groups=mesh['dp'=8,'segment'=4] {'dp','segment'}, use_global_device_ids=true, to_apply=%region_1.0 | all-reduce | flops 15360 | bytes 122880 | tf_op jit(solution)/shard_map/psum | solution.py:213
  53.1 37.4 %while.85 = (s32[]{:T(128)}, bf16[1,64,640]{2,1,0:T(8,128)(2,1)S(1)}, bf16[3,64,640]{2,1,0:T(8,128)(2,1)S(1)}, bf16[3,64,640]{2,1,0:T(8,128)(2,1)S(1)}, bf16[3,6...) while((s32[]{:T(128)}, ...), condition=%wide.region_9.10_spmd, body=%wide.region_2.9_spmd.sunk | while | flops 158269488 | bytes 4230608 | solution.py:247
  54.1 5.1 conditional.11
  55.7 2.3 fusion.1
  62.6 5.1 conditional.11
  64.2 2.3 fusion.1
  67.6 2.3 collective-permute-start
  72.0 5.1 conditional.11
  73.7 2.3 fusion.1
  77.1 2.6 collective-permute-start
  82.5 7.0 %collective-permute-start = (bf16[1,64,640]{2,1,0:T(8,128)(2,1)}, bf16[1,64,640]{2,1,0:T(8,128)(2,1)S(1)}, u32[]{:S(2)}, u32[]{:S(2)}) collective-permute-start(bf16[1,64,640]{2,1,0:T(8,128)(2,1)} %get-tuple-element.2083), channel_id=1, source_target_pairs={{0,1},{1,2},{2,3},{4,5},{5,6},{6,7},{8,9},{9,10},{10,11},{12,13},{... | collective-permute-start | bytes 245768 | tf_op jit(solution)/shard_map/while/body/eval_jaxpr/ppermute | solution.py:17
  92.5 2.5 collective-permute-start.5
  95.0 6.4 %collective-permute-done.5 = bf16[3,64,640]{2,1,0:T(8,128)(2,1)} collective-permute-done((bf16[3,64,640]{2,1,0:T(8,128)(2,1)S(1)}, bf16[3,64,640]{2,1,0:T(8,128)(2,1)}, u32[]{:S(2)}, u32[]{:S(2)}) %collective-permute-start.5) | collective-permute-done | bytes 245792 | tf_op jit(solution)/shard_map/ppermute | solution.py:27
  101.4 22.9 %while.86 = (s32[]{:T(128)}, bf16[1,64,640]{2,1,0:T(8,128)(2,1)S(1)}, bf16[3,64,640]{2,1,0:T(8,128)(2,1)S(1)}, s32[]{:T(128)}, pred[]{:T(512)}, /*index=5*/pred[...) while((s32[]{:T(128)}, ...), condition=%wide.region_17.18_spmd, body=%wide.region_10.17_spmd.sunk | while | flops 158064688 | bytes 3984758 | solution.py:278
  104.0 9.1 %collective-permute-start.1 = (bf16[1,64,640]{2,1,0:T(8,128)(2,1)S(1)}, bf16[1,64,640]{2,1,0:T(8,128)(2,1)S(1)}, u32[]{:S(2)}, u32[]{:S(2)}) collective-permute-start(bf16[1,64,640]{2,1,0:T(8,128)(2,1)S(1)} %get-tuple-element.2400), channel_id=1, source_target_pairs={{0,1},{1,2},{2,3},{4,5},{5,6},{6,7},{8,9},{9,10},{10,11},{12,13},{... | collective-permute-start | bytes 245768 | tf_op jit(solution)/shard_map/while/body/eval_jaxpr/ppermute | solution.py:17
  114.1 9.2 %collective-permute-start.1 = (bf16[1,64,640]{2,1,0:T(8,128)(2,1)S(1)}, bf16[1,64,640]{2,1,0:T(8,128)(2,1)S(1)}, u32[]{:S(2)}, u32[]{:S(2)}) collective-permute-start(bf16[1,64,640]{2,1,0:T(8,128)(2,1)S(1)} %get-tuple-element.2400), channel_id=1, source_target_pairs={{0,1},{1,2},{2,3},{4,5},{5,6},{6,7},{8,9},{9,10},{10,11},{12,13},{... | collective-permute-start | bytes 245768 | tf_op jit(solution)/shard_map/while/body/eval_jaxpr/ppermute | solution.py:17
  126.3 81.1 %while.88 = (s32[]{:T(128)}, bf16[1,64,640]{2,1,0:T(8,128)(2,1)}, f32[640,640]{1,0:T(8,128)}, f32[640,640]{1,0:T(8,128)}, f32[640,640]{1,0:T(8,128)}, /*index=5*...) while((s32[]{:T(128)}, bf16[1,64,640]{2,1,0:T(8,128)(2,1)}, ...), condition=%wide.region_29.30_spmd.clone, body=%wide.region_18.29_spmd.clone.sunk | while | flops 423731232 | bytes 37466964 | solution.py:318
  126.3 5.2 %conditional.14 = (bf16[1,64,640]{2,1,0:T(8,128)(2,1)}, bf16[1,64,640]{2,1,0:T(8,128)(2,1)}, f32[640,640]{1,0:T(8,128)}, f32[640,640]{1,0:T(8,128)}, f32[640,640]{1,0:T(8,128)}) conditional(s32[]{:T(128)} %convert_element_type.389, () %tuple.224, (pred[]{:T(512)}, bf16[3,64,640]{2,1,0:T(8,128)(2,1)}, s32[]{:T(128)}, ...), branch_computations={%region_19.19_spmd, %region_20.28_spmd} | conditional | flops 421191712 | bytes 17641720 | solution.py:308
  132.9 2.8 select_add_fusion.5
  135.7 4.0 select_add_fusion.6
  139.7 2.0 collective-permute-done.3
  142.5 5.2 %conditional.14 = (bf16[1,64,640]{2,1,0:T(8,128)(2,1)}, bf16[1,64,640]{2,1,0:T(8,128)(2,1)}, f32[640,640]{1,0:T(8,128)}, f32[640,640]{1,0:T(8,128)}, f32[640,640]{1,0:T(8,128)}) conditional(s32[]{:T(128)} %convert_element_type.389, () %tuple.224, (pred[]{:T(512)}, bf16[3,64,640]{2,1,0:T(8,128)(2,1)}, s32[]{:T(128)}, ...), branch_computations={%region_19.19_spmd, %region_20.28_spmd} | conditional | flops 421191712 | bytes 17641720 | solution.py:308
  149.0 3.3 select_add_fusion.5
  152.3 5.0 select_add_fusion.6
  158.1 5.2 %conditional.14 = (bf16[1,64,640]{2,1,0:T(8,128)(2,1)}, bf16[1,64,640]{2,1,0:T(8,128)(2,1)}, f32[640,640]{1,0:T(8,128)}, f32[640,640]{1,0:T(8,128)}, f32[640,640]{1,0:T(8,128)}) conditional(s32[]{:T(128)} %convert_element_type.389, () %tuple.224, (pred[]{:T(512)}, bf16[3,64,640]{2,1,0:T(8,128)(2,1)}, s32[]{:T(128)}, ...), branch_computations={%region_19.19_spmd, %region_20.28_spmd} | conditional | flops 421191712 | bytes 17641720 | solution.py:308
  164.7 3.3 select_add_fusion.5
  168.0 5.0 select_add_fusion.6
  173.0 6.7 %collective-permute-done.3 = bf16[1,64,640]{2,1,0:T(8,128)(2,1)S(1)} collective-permute-done((bf16[1,64,640]{2,1,0:T(8,128)(2,1)}, bf16[1,64,640]{2,1,0:T(8,128)(2,1)S(1)}, u32[]{:S(2)}, u32[]{:S(2)}) %collective-permute-start.3) | collective-permute-done | bytes 81952 | tf_op jit(solution)/shard_map/while/body/eval_jaxpr/ppermute | solution.py:17
  180.4 5.2 %conditional.14 = (bf16[1,64,640]{2,1,0:T(8,128)(2,1)}, bf16[1,64,640]{2,1,0:T(8,128)(2,1)}, f32[640,640]{1,0:T(8,128)}, f32[640,640]{1,0:T(8,128)}, f32[640,640]{1,0:T(8,128)}) conditional(s32[]{:T(128)} %convert_element_type.389, () %tuple.224, (pred[]{:T(512)}, bf16[3,64,640]{2,1,0:T(8,128)(2,1)}, s32[]{:T(128)}, ...), branch_computations={%region_19.19_spmd, %region_20.28_spmd} | conditional | flops 421191712 | bytes 17641720 | solution.py:308
  186.9 3.3 select_add_fusion.5
  190.2 5.0 select_add_fusion.6
  195.3 11.4 %collective-permute-done.3 = bf16[1,64,640]{2,1,0:T(8,128)(2,1)S(1)} collective-permute-done((bf16[1,64,640]{2,1,0:T(8,128)(2,1)}, bf16[1,64,640]{2,1,0:T(8,128)(2,1)S(1)}, u32[]{:S(2)}, u32[]{:S(2)}) %collective-permute-start.3) | collective-permute-done | bytes 81952 | tf_op jit(solution)/shard_map/while/body/eval_jaxpr/ppermute | solution.py:17
  207.4 18.2 %collective-permute-start.6 = (bf16[3,64,640]{2,1,0:T(8,128)(2,1)}, bf16[3,64,640]{2,1,0:T(8,128)(2,1)S(1)}, u32[]{:S(2)}, u32[]{:S(2)}) collective-permute-start(bf16[3,64,640]{2,1,0:T(8,128)(2,1)} %get-tuple-element.1548), channel_id=1, source_target_pairs={{0,1},{1,0},{2,3},{3,2},{4,5},{5,4},{6,7},{7,6},{8,9},{9,8},{10,11... | collective-permute-start | bytes 737288 | tf_op jit(solution)/shard_map/ppermute | solution.py:27
  227.0 7.2 %collective-permute-start.7 = (bf16[3,64,640]{2,1,0:T(8,128)(2,1)S(1)}, bf16[3,64,640]{2,1,0:T(8,128)(2,1)}, u32[]{:S(2)}, u32[]{:S(2)}) collective-permute-start(bf16[3,64,640]{2,1,0:T(8,128)(2,1)S(1)} %collective-permute-done.6), channel_id=1, source_target_pairs={{0,2},{2,0},{1,3},{3,1},{4,6},{6,4},{5,7},{7,5},{8,10},{10,8},{9,1... | collective-permute-start | bytes 737288 | tf_op jit(solution)/shard_map/ppermute | solution.py:27
  234.2 6.4 %collective-permute-done.7 = bf16[3,64,640]{2,1,0:T(8,128)(2,1)} collective-permute-done((bf16[3,64,640]{2,1,0:T(8,128)(2,1)S(1)}, bf16[3,64,640]{2,1,0:T(8,128)(2,1)}, u32[]{:S(2)}, u32[]{:S(2)}) %collective-permute-start.7) | collective-permute-done | bytes 245792 | tf_op jit(solution)/shard_map/ppermute | solution.py:27
  241.2 69.8 %while.87 = (s32[]{:T(128)}, bf16[1,64,640]{2,1,0:T(8,128)(2,1)}, f32[640,640]{1,0:T(8,128)}, f32[640,640]{1,0:T(8,128)}, f32[640,640]{1,0:T(8,128)}, /*index=5*...) while((s32[]{:T(128)}, bf16[1,64,640]{2,1,0:T(8,128)(2,1)}, ...), condition=%wide.region_41.42_spmd, body=%wide.region_30.41_spmd.sunk | while | flops 422993952 | bytes 31823388 | solution.py:360
  241.2 4.6 conditional.13
  247.1 3.3 add.598
  250.4 3.3 add.599
  253.6 3.3 add.600
  258.3 14.0 %conditional.13 = (bf16[1,64,640]{2,1,0:T(8,128)(2,1)}, f32[640,640]{1,0:T(8,128)}, f32[640,640]{1,0:T(8,128)}, f32[640,640]{1,0:T(8,128)}) conditional(s32[]{:T(128)} %convert_element_type.388, () %tuple.220, (pred[]{:T(512)}, s32[]{:T(128)}, bf16[3,64,640]{2,1,0:T(8,128)(2,1)}, bf16[1,64,640]{2,1,0:T(8,128)(2,1)}, ...), branch_computations={%region_31.31_spmd, %region_32.40_spmd} | conditional | flops 421765152 | bytes 16422076 | solution.py:350
  262.6 1.6 fusion.86
  265.8 2.8 fusion.65
  270.7 1.6 fusion.76
  273.6 3.3 add.598
  276.9 3.3 add.599
  280.2 3.3 add.600
  284.7 14.0 %conditional.13 = (bf16[1,64,640]{2,1,0:T(8,128)(2,1)}, f32[640,640]{1,0:T(8,128)}, f32[640,640]{1,0:T(8,128)}, f32[640,640]{1,0:T(8,128)}) conditional(s32[]{:T(128)} %convert_element_type.388, () %tuple.220, (pred[]{:T(512)}, s32[]{:T(128)}, bf16[3,64,640]{2,1,0:T(8,128)(2,1)}, bf16[1,64,640]{2,1,0:T(8,128)(2,1)}, ...), branch_computations={%region_31.31_spmd, %region_32.40_spmd} | conditional | flops 421765152 | bytes 16422076 | solution.py:350
  289.0 1.6 fusion.86
  292.2 2.8 fusion.65
  297.1 1.6 fusion.76
  300.0 3.3 add.598
  303.3 3.3 add.599
  306.5 3.3 add.600
  311.0 9.6 %conditional.5 = (f32[640,640]{1,0:T(8,128)}, f32[640,640]{1,0:T(8,128)}, f32[640,640]{1,0:T(8,128)}) conditional(s32[]{:T(128)} %convert_element_type.224, () %tuple.155, (s32[]{:T(128)}, bf16[3,64,640]{2,1,0:T(8,128)(2,1)S(1)}, pred[]{:T(512)}, bf16[3,64,640]{2,1,0:T(8,128)(2,1)}, bf16[1,64,640]{2,1,0:T(8,128)(2,1)}, ...), branch_computations={%region_42.43_spmd, %region_43.48_spmd} | conditional | flops 368680992 | bytes 13174888 | solution.py:350
  314.4 1.6 fusion.132
  316.0 1.9 fusion.103
  317.9 2.8 fusion.106
  320.7 3.0 add_convert_fusion
  323.7 3.1 add_convert_fusion.1
  326.9 2.5 add_convert_fusion.2
  329.4 56.6 %reduce-scatter.8.cloned.1.call-done = bf16[80,640]{1,0:T(8,128)(2,1)} async-done(((bf16[640,640]{1,0:T(8,128)(2,1)}), bf16[80,640]{1,0:T(8,128)(2,1)}) %reduce-scatter.8.cloned.1.call-update) | async-done | bytes 102416 | tf_op jit(solution)/shard_map/reduce_scatter | solution.py:369
  387.5 58.8 %reduce-scatter.6.cloned.1.call-done = bf16[80,640]{1,0:T(8,128)(2,1)} async-done(((bf16[640,640]{1,0:T(8,128)(2,1)}), bf16[80,640]{1,0:T(8,128)(2,1)}) %reduce-scatter.6.cloned.1.call-update) | async-done | bytes 102416 | tf_op jit(solution)/shard_map/reduce_scatter | solution.py:366
  447.9 59.0 %reduce-scatter.4.cloned.1.call-done = bf16[80,640]{1,0:T(8,128)(2,1)} async-done(((bf16[640,640]{1,0:T(8,128)(2,1)}), bf16[80,640]{1,0:T(8,128)(2,1)}) %reduce-scatter.4.cloned.1.call-update) | async-done | bytes 102416 | tf_op jit(solution)/shard_map/reduce_scatter | solution.py:363
  (291 shorter events, 97.9 us)
Async XLA Ops:
  7.2 1.5 copy-start
  7.2 45.9 %copy-start.2 = (bf16[1,640,640]{2,1,0:T(8,128)(2,1)S(1)}, bf16[1,640,640]{2,1,0:T(8,128)(2,1)}, u32[]{:S(2)}) copy-start(bf16[1,640,640]{2,1,0:T(8,128)(2,1)} %param.30) | copy-start | bytes 2457604
  7.2 45.9 %copy-start.1 = (bf16[1,640,640]{2,1,0:T(8,128)(2,1)S(1)}, bf16[1,640,640]{2,1,0:T(8,128)(2,1)}, u32[]{:S(2)}) copy-start(bf16[1,640,640]{2,1,0:T(8,128)(2,1)} %param.32) | copy-start | bytes 2457604
  7.2 378.8 %reduce-scatter.8.cloned.1.call-start = ((), (), s32[]{:S(2)}) async-start(), calls=%async_computation.5 | async-start | bytes 921600 | tf_op jit(solution)/shard_map/reduce_scatter | solution.py:369
  59.2 2.4 collective-permute-start
  67.6 3.4 collective-permute-start
  77.1 3.7 collective-permute-start
  82.5 8.1 %collective-permute-start = (bf16[1,64,640]{2,1,0:T(8,128)(2,1)}, bf16[1,64,640]{2,1,0:T(8,128)(2,1)S(1)}, u32[]{:S(2)}, u32[]{:S(2)}) collective-permute-start(bf16[1,64,640]{2,1,0:T(8,128)(2,1)} %get-tuple-element.2083), channel_id=1, source_target_pairs={{0,1},{1,2},{2,3},{4,5},{5,6},{6,7},{8,9},{9,10},{10,11},{12,13},{... | collective-permute-start | bytes 245768 | tf_op jit(solution)/shard_map/while/body/eval_jaxpr/ppermute | solution.py:17
  90.6 1.9 collective-permute-start.4
  92.5 8.9 %collective-permute-start.5 = (bf16[3,64,640]{2,1,0:T(8,128)(2,1)S(1)}, bf16[3,64,640]{2,1,0:T(8,128)(2,1)}, u32[]{:S(2)}, u32[]{:S(2)}) collective-permute-start(bf16[3,64,640]{2,1,0:T(8,128)(2,1)S(1)} %collective-permute-done.4), channel_id=1, source_target_pairs={{0,2},{2,0},{1,3},{3,1},{4,6},{6,4},{5,7},{7,5},{8,10},{10,8},{9,1... | collective-permute-start | bytes 737288 | tf_op jit(solution)/shard_map/ppermute | solution.py:27
  101.5 2.4 collective-permute-start.1
  104.0 10.1 %collective-permute-start.1 = (bf16[1,64,640]{2,1,0:T(8,128)(2,1)S(1)}, bf16[1,64,640]{2,1,0:T(8,128)(2,1)S(1)}, u32[]{:S(2)}, u32[]{:S(2)}) collective-permute-start(bf16[1,64,640]{2,1,0:T(8,128)(2,1)S(1)} %get-tuple-element.2400), channel_id=1, source_target_pairs={{0,1},{1,2},{2,3},{4,5},{5,6},{6,7},{8,9},{9,10},{10,11},{12,13},{... | collective-permute-start | bytes 245768 | tf_op jit(solution)/shard_map/while/body/eval_jaxpr/ppermute | solution.py:17
  114.1 10.1 %collective-permute-start.1 = (bf16[1,64,640]{2,1,0:T(8,128)(2,1)S(1)}, bf16[1,64,640]{2,1,0:T(8,128)(2,1)S(1)}, u32[]{:S(2)}, u32[]{:S(2)}) collective-permute-start(bf16[1,64,640]{2,1,0:T(8,128)(2,1)S(1)} %get-tuple-element.2400), channel_id=1, source_target_pairs={{0,1},{1,2},{2,3},{4,5},{5,6},{6,7},{8,9},{9,10},{10,11},{12,13},{... | collective-permute-start | bytes 245768 | tf_op jit(solution)/shard_map/while/body/eval_jaxpr/ppermute | solution.py:17
  131.6 10.2 %collective-permute-start.3 = (bf16[1,64,640]{2,1,0:T(8,128)(2,1)}, bf16[1,64,640]{2,1,0:T(8,128)(2,1)S(1)}, u32[]{:S(2)}, u32[]{:S(2)}) collective-permute-start(bf16[1,64,640]{2,1,0:T(8,128)(2,1)} %get-tuple-element.2137), channel_id=1, source_target_pairs={{1,0},{2,1},{3,2},{5,4},{6,5},{7,6},{9,8},{10,9},{11,10},{13,12},{... | collective-permute-start | bytes 245768 | tf_op jit(solution)/shard_map/while/body/eval_jaxpr/ppermute | solution.py:17
  135.7 4.0 copy-start.17
  135.7 6.1 %copy-start.14 = (bf16[3,64,640]{2,1,0:T(8,128)(2,1)S(1)}, bf16[3,64,640]{2,1,0:T(8,128)(2,1)}, u32[]{:S(2)}) copy-start(bf16[3,64,640]{2,1,0:T(8,128)(2,1)} %get-tuple-element.2300) | copy-start | bytes 737284 | tf_op jit(solution)/shard_map/while
  139.7 2.1 copy-start.18
  141.8 0.6 copy-start.12
  141.8 0.7 copy-start.15
  147.7 9.6 %collective-permute-start.3 = (bf16[1,64,640]{2,1,0:T(8,128)(2,1)}, bf16[1,64,640]{2,1,0:T(8,128)(2,1)S(1)}, u32[]{:S(2)}, u32[]{:S(2)}) collective-permute-start(bf16[1,64,640]{2,1,0:T(8,128)(2,1)} %get-tuple-element.2137), channel_id=1, source_target_pairs={{1,0},{2,1},{3,2},{5,4},{6,5},{7,6},{9,8},{10,9},{11,10},{13,12},{... | collective-permute-start | bytes 245768 | tf_op jit(solution)/shard_map/while/body/eval_jaxpr/ppermute | solution.py:17
  152.3 5.0 copy-start.17
  152.3 5.1 copy-start.14
  157.3 0.7 copy-start.18
  157.4 0.7 copy-start.12
  157.4 0.7 copy-start.15
  163.4 16.3 %collective-permute-start.3 = (bf16[1,64,640]{2,1,0:T(8,128)(2,1)}, bf16[1,64,640]{2,1,0:T(8,128)(2,1)S(1)}, u32[]{:S(2)}, u32[]{:S(2)}) collective-permute-start(bf16[1,64,640]{2,1,0:T(8,128)(2,1)} %get-tuple-element.2137), channel_id=1, source_target_pairs={{1,0},{2,1},{3,2},{5,4},{6,5},{7,6},{9,8},{10,9},{11,10},{13,12},{... | collective-permute-start | bytes 245768 | tf_op jit(solution)/shard_map/while/body/eval_jaxpr/ppermute | solution.py:17
  168.0 5.0 copy-start.17
  168.0 11.7 %copy-start.14 = (bf16[3,64,640]{2,1,0:T(8,128)(2,1)S(1)}, bf16[3,64,640]{2,1,0:T(8,128)(2,1)}, u32[]{:S(2)}) copy-start(bf16[3,64,640]{2,1,0:T(8,128)(2,1)} %get-tuple-element.2300) | copy-start | bytes 737284 | tf_op jit(solution)/shard_map/while
  173.0 6.7 %copy-start.18 = (bf16[3,64,640]{2,1,0:T(8,128)(2,1)}, bf16[3,64,640]{2,1,0:T(8,128)(2,1)S(1)}, u32[]{:S(2)}) copy-start(bf16[3,64,640]{2,1,0:T(8,128)(2,1)S(1)} %select_dynamic-update-slice_fusion.17) | copy-start | bytes 737284 | tf_op jit(solution)/shard_map/while
  179.7 0.6 copy-start.12
  179.7 0.7 copy-start.15
  185.7 21.1 %collective-permute-start.3 = (bf16[1,64,640]{2,1,0:T(8,128)(2,1)}, bf16[1,64,640]{2,1,0:T(8,128)(2,1)S(1)}, u32[]{:S(2)}, u32[]{:S(2)}) collective-permute-start(bf16[1,64,640]{2,1,0:T(8,128)(2,1)} %get-tuple-element.2137), channel_id=1, source_target_pairs={{1,0},{2,1},{3,2},{5,4},{6,5},{7,6},{9,8},{10,9},{11,10},{13,12},{... | collective-permute-start | bytes 245768 | tf_op jit(solution)/shard_map/while/body/eval_jaxpr/ppermute | solution.py:17
  190.2 5.0 copy-start.17
  190.2 16.5 %copy-start.14 = (bf16[3,64,640]{2,1,0:T(8,128)(2,1)S(1)}, bf16[3,64,640]{2,1,0:T(8,128)(2,1)}, u32[]{:S(2)}) copy-start(bf16[3,64,640]{2,1,0:T(8,128)(2,1)} %get-tuple-element.2300) | copy-start | bytes 737284 | tf_op jit(solution)/shard_map/while
  195.3 11.5 %copy-start.18 = (bf16[3,64,640]{2,1,0:T(8,128)(2,1)}, bf16[3,64,640]{2,1,0:T(8,128)(2,1)S(1)}, u32[]{:S(2)}) copy-start(bf16[3,64,640]{2,1,0:T(8,128)(2,1)S(1)} %select_dynamic-update-slice_fusion.17) | copy-start | bytes 737284 | tf_op jit(solution)/shard_map/while
  206.7 0.6 copy-start.12
  206.8 0.7 copy-start.15
  207.4 19.5 %collective-permute-start.6 = (bf16[3,64,640]{2,1,0:T(8,128)(2,1)}, bf16[3,64,640]{2,1,0:T(8,128)(2,1)S(1)}, u32[]{:S(2)}, u32[]{:S(2)}) collective-permute-start(bf16[3,64,640]{2,1,0:T(8,128)(2,1)} %get-tuple-element.1548), channel_id=1, source_target_pairs={{0,1},{1,0},{2,3},{3,2},{4,5},{5,4},{6,7},{7,6},{8,9},{9,8},{10,11... | collective-permute-start | bytes 737288 | tf_op jit(solution)/shard_map/ppermute | solution.py:27
  227.0 13.6 %collective-permute-start.7 = (bf16[3,64,640]{2,1,0:T(8,128)(2,1)S(1)}, bf16[3,64,640]{2,1,0:T(8,128)(2,1)}, u32[]{:S(2)}, u32[]{:S(2)}) collective-permute-start(bf16[3,64,640]{2,1,0:T(8,128)(2,1)S(1)} %collective-permute-done.6), channel_id=1, source_target_pairs={{0,2},{2,0},{1,3},{3,1},{4,6},{6,4},{5,7},{7,5},{8,10},{10,8},{9,1... | collective-permute-start | bytes 737288 | tf_op jit(solution)/shard_map/ppermute | solution.py:27
  245.8 11.8 %collective-permute-start.2 = (bf16[1,64,640]{2,1,0:T(8,128)(2,1)}, bf16[1,64,640]{2,1,0:T(8,128)(2,1)S(1)}, u32[]{:S(2)}, u32[]{:S(2)}) collective-permute-start(bf16[1,64,640]{2,1,0:T(8,128)(2,1)} %get-tuple-element.2115), channel_id=1, source_target_pairs={{1,0},{2,1},{3,2},{5,4},{6,5},{7,6},{9,8},{10,9},{11,10},{13,12},{... | collective-permute-start | bytes 245768 | tf_op jit(solution)/shard_map/while/body/eval_jaxpr/ppermute | solution.py:17
  257.7 0.6 copy-start.16
  258.3 3.3 copy-start.5
  261.5 2.7 copy-start.7
  261.9 0.6 copy-start.13
  272.3 11.7 %collective-permute-start.2 = (bf16[1,64,640]{2,1,0:T(8,128)(2,1)}, bf16[1,64,640]{2,1,0:T(8,128)(2,1)S(1)}, u32[]{:S(2)}, u32[]{:S(2)}) collective-permute-start(bf16[1,64,640]{2,1,0:T(8,128)(2,1)} %get-tuple-element.2115), channel_id=1, source_target_pairs={{1,0},{2,1},{3,2},{5,4},{6,5},{7,6},{9,8},{10,9},{11,10},{13,12},{... | collective-permute-start | bytes 245768 | tf_op jit(solution)/shard_map/while/body/eval_jaxpr/ppermute | solution.py:17
  284.0 0.6 copy-start.16
  284.7 3.3 copy-start.5
  287.9 2.7 copy-start.7
  288.3 0.6 copy-start.13
  298.7 11.7 %collective-permute-start.2 = (bf16[1,64,640]{2,1,0:T(8,128)(2,1)}, bf16[1,64,640]{2,1,0:T(8,128)(2,1)S(1)}, u32[]{:S(2)}, u32[]{:S(2)}) collective-permute-start(bf16[1,64,640]{2,1,0:T(8,128)(2,1)} %get-tuple-element.2115), channel_id=1, source_target_pairs={{1,0},{2,1},{3,2},{5,4},{6,5},{7,6},{9,8},{10,9},{11,10},{13,12},{... | collective-permute-start | bytes 245768 | tf_op jit(solution)/shard_map/while/body/eval_jaxpr/ppermute | solution.py:17
  310.4 0.6 copy-start.16
  312.9 3.1 copy-start.6
  323.6 122.7 %reduce-scatter.6.cloned.1.call-start = ((), (), s32[]{:S(2)}) async-start(), calls=%async_computation.4 | async-start | bytes 921600 | tf_op jit(solution)/shard_map/reduce_scatter | solution.py:366
  323.7 3.2 copy-start.3
  326.8 180.0 %reduce-scatter.4.cloned.1.call-start = ((), (), s32[]{:S(2)}) async-start(), calls=%async_computation.3 | async-start | bytes 921600 | tf_op jit(solution)/shard_map/reduce_scatter | solution.py:363
Sparse Core Ops, SparseCore 0:
  323.8 62.1 reduce-scatter.7
  389.3 56.9 reduce-scatter.5
  449.7 57.1 reduce-scatter.3
where the time goes:
time: 517 us; the launch traced here: 515 us
  waiting for transfers between devices  219 us (42%)
  other arithmetic  87.2 us (17%)
  starting transfers between devices  70.7 us (14%)
  local copies, waits for them, and re-layouts  43.7 us (8%)
  blocking collectives  42.6 us (8%)
  matrix products  37 us (7%)
  between operations  13.9 us (3%)
    reduce_scatter x1, waiting for transfers between devices, on_device(): lax.psum_scatter(grad_sums[0].astype(jnp.bfloat16), 'dp', scatter_dimensi...  59 us
    reduce_scatter x1, waiting for transfers between devices, on_device(): lax.psum_scatter(grad_sums[1].astype(jnp.bfloat16), 'dp', scatter_dimensi...  58.8 us
    reduce_scatter x1, waiting for transfers between devices, on_device(): lax.psum_scatter(grad_sums[2].astype(jnp.bfloat16), 'dp', scatter_dimensi...  56.6 us
    psum x1, blocking collectives, on_device(): pooled_all = lax.psum(partial_sum, ('dp', 'segment'))  42.6 us
    ppermute x14, starting transfers between devices, shifted_2(): lax.ppermute(value, axis, [(source, source + steps) for source in range(i...  41.9 us
    add x8, other arithmetic, dec_back_step(): grad_sums = tuple((old + new for old, new in zip(grad_sums, new_grads)))  31.6 us
    add x9, other arithmetic, enc_back_compute(): grad_sums = tuple((old + new for old, new in zip(grad_sums, new_grads)))  29.4 us
    ppermute x14, waiting for transfers between devices, shifted_2(): lax.ppermute(value, axis, [(source, source + steps) for source in range(i...  29 us
  transfers between devices with their start and end apart: 21, of which 20 were waited for; matrix products, arithmetic and copies ran while one was open for 14% of the time, Pallas kernels for 0%

commit v1 on v0

v1 whole, which is shorter than its diff:
```python
import functools
import math

import jax
import jax.numpy as jnp
from jax import lax
from jax.experimental import pallas as pl
from jax.experimental.pallas import tpu as pltpu
from jax.sharding import PartitionSpec as P

GROUPS = 32
EPSILON = 1e-05
F32 = jnp.float32
BF16 = jnp.bfloat16


def dot(left, right):
    return jnp.dot(left, right, preferred_element_type=F32)


def dot_t(left, right):
    return lax.dot_general(left, right, (((1,), (1,)), ((), ())), preferred_element_type=F32)


def dot_tn(left, right):
    return lax.dot_general(left, right, (((0,), (0,)), ((), ())), preferred_element_type=F32)


def group_sum(rows, members):
    count = rows.shape[0]
    high = rows.astype(BF16)
    rest = rows - high.astype(F32)
    middle = rest.astype(BF16)
    low = (rest - middle.astype(F32)).astype(BF16)
    total = dot(jnp.concatenate([high, middle, low], axis=0), members)
    return total[:count] + total[count : 2 * count] + total[2 * count :]


def pad_rows(rows):
    extra = -rows.shape[0] % 8
    if extra == 0:
        return rows
    return jnp.concatenate([rows, jnp.zeros((extra, rows.shape[1]), F32)], axis=0)


def norm(block, members, count):
    channels = block.shape[-1]
    rows = block.shape[0] // count
    share = 1.0 / (rows * (channels // GROUPS))
    split = block.reshape(count, rows, channels)
    center = group_sum(pad_rows(jnp.sum(split, axis=1)), members) * share
    shifted = split - center[:count][:, None, :]
    spread = group_sum(pad_rows(jnp.sum(shifted * shifted, axis=1)), members) * share
    inv_scale = lax.rsqrt(spread + EPSILON)
    return shifted * inv_scale[:count][:, None, :], center, inv_scale


def norm_back(grad, normed, inv_scale, members, count):
    channels = grad.shape[-1]
    rows = grad.shape[0] // count
    share = 1.0 / (rows * (channels // GROUPS))
    split = grad.reshape(count, rows, channels)
    sums = jnp.concatenate([jnp.sum(split, axis=1), jnp.sum(split * normed, axis=1)], axis=0)
    means = group_sum(pad_rows(sums), members) * share
    first = means[:count][:, None, :]
    second = means[count : 2 * count][:, None, :]
    back = inv_scale[:count][:, None, :] * (split - first - normed * second)
    return back.reshape(grad.shape)


def activate(pre_act):
    sig = jax.nn.sigmoid(pre_act)
    hidden = (pre_act * sig).astype(BF16)
    slope = sig * (1.0 + pre_act * (1.0 - sig))
    return hidden, slope


def block_pre_act(normed_low, weight, cond, count):
    pre_act = dot(normed_low, weight)
    rows = pre_act.shape[0] // count
    return (
        pre_act.reshape(count, rows, -1) + cond[:count][:, None, :]
    ).reshape(pre_act.shape)


def as_low(normed):
    count, rows, channels = normed.shape
    return normed.reshape(count * rows, channels).astype(BF16)


class Loader:
    def __init__(self, core, sems):
        self.core, self.sems, self.used = core, sems, 0

    def pair(self, own, other, slots):
        copies = (
            pltpu.make_async_copy(own, slots.at[self.core], self.sems.at[self.used]),
            pltpu.make_async_copy(other, slots.at[1 - self.core], self.sems.at[self.used + 1]),
        )
        self.used += 2
        for copy in copies:
            copy.start()
        return lambda: [copy.wait() for copy in copies]


def enc_fwd_kernel(
    count, core_ref, x_ref, cond_ref, members_ref, own_in, oth_in, own_out, oth_out,
    x1_ref, x2_ref, hid_ref, low_ref, slope0_ref, slope1_ref, stat_ref, low0_ref,
    w_in, w_out, sems,
):
    core = core_ref[0]
    loader = Loader(core, sems)
    in_ready = loader.pair(own_in, oth_in, w_in)
    out_ready = loader.pair(own_out, oth_out, w_out)
    members = members_ref[...]
    cond = cond_ref[...]

    x0 = x_ref[...].astype(F32)
    normed, center0, scale0 = norm(x0, members, count)
    low0 = as_low(normed)
    in_ready()
    hid0, slope0 = activate(block_pre_act(low0, w_in[0], cond, count))
    slope0_ref[...] = slope0
    out_ready()
    x1 = (x0 + dot(hid0, w_out[0])).astype(BF16)
    x1_ref[...] = x1

    x1 = x1.astype(F32)
    normed, center1, scale1 = norm(x1, members, count)
    low1 = as_low(normed)
    hid1, slope1 = activate(block_pre_act(low1, w_in[1], cond, count))
    slope1_ref[...] = slope1
    x2_ref[...] = (x1 + dot(hid1, w_out[1])).astype(BF16)

    stat_ref[0] = center0
    stat_ref[1] = scale0
    stat_ref[2] = center1
    stat_ref[3] = scale1
    even = core == 0
    hid_ref[...] = jnp.where(even, hid0, hid1)
    low_ref[...] = jnp.where(even, low0, low1)


def dec_kernel(
    count, combine, core_ref, x_ref, m0_ref, m1_ref, cond_ref, d_ref, members_ref,
    own_in, oth_in, own_out, oth_out, own_skip, oth_skip, own_mir, oth_mir,
    down_ref, high_ref, low_back_ref,
    l_out_ref, r_out_ref, l_in_ref, r_in_ref, l_skip_ref, r_skip_ref, l_mir_ref, r_mir_ref,
    w_in, w_out, w_skip, w_mir, sems,
):
    core = core_ref[0]
    loader = Loader(core, sems)
    mir_ready = loader.pair(own_mir, oth_mir, w_mir)
    skip_ready = loader.pair(own_skip, oth_skip, w_skip)
    in_ready = loader.pair(own_in, oth_in, w_in)
    out_ready = loader.pair(own_out, oth_out, w_out)
    members = members_ref[...]
    cond = cond_ref[...]
    m0 = m0_ref[...]
    m1 = m1_ref[...]
    d_in = d_ref[...]

    mir_ready()
    skip_e = dot(m1, w_mir[1]).astype(BF16)
    skip_o = dot(m0, w_mir[0]).astype(BF16)
    skip_ready()
    z_e = x_ref[...].astype(F32) + dot(skip_e, w_skip[0])
    norm_e, _, scale_e = norm(z_e, members, count)
    low_e = as_low(norm_e)
    in_ready()
    hid_e, slope_e = activate(block_pre_act(low_e, w_in[0], cond, count))
    out_ready()
    x_o = (z_e + dot(hid_e, w_out[0])).astype(BF16)

    z_o = x_o.astype(F32) + dot(skip_o, w_skip[1])
    norm_o, _, scale_o = norm(z_o, members, count)
    low_o = as_low(norm_o)
    hid_o, slope_o = activate(block_pre_act(low_o, w_in[1], cond, count))

    e_o = (dot_t(d_in, w_out[1]) * slope_o).astype(BF16)
    back_o = norm_back(dot_t(e_o, w_in[1]), norm_o, scale_o, members, count)
    g_o = (d_in.astype(F32) + back_o).astype(BF16)

    e_e = (dot_t(g_o, w_out[0]) * slope_e).astype(BF16)
    back_e = norm_back(dot_t(e_e, w_in[0]), norm_e, scale_e, members, count)
    g_e = (g_o.astype(F32) + back_e).astype(BF16)

    q_e = dot_t(g_e, w_skip[0]).astype(BF16)
    high = dot_t(q_e, w_mir[1])
    if combine:
        down_ref[...] = (g_e.astype(F32) + high).astype(BF16)
    else:
        down_ref[...] = g_e
        high_ref[...] = high.astype(BF16)
    q_o = dot_t(g_o, w_skip[1]).astype(BF16)
    low_back_ref[...] = dot_t(q_o, w_mir[0]).astype(BF16)

    even = core == 0
    l_out_ref[...] = jnp.where(even, hid_e, hid_o)
    r_out_ref[...] = jnp.where(even, g_o, d_in)
    l_in_ref[...] = jnp.where(even, low_e, low_o)
    r_in_ref[...] = jnp.where(even, e_e, e_o)
    l_skip_ref[...] = jnp.where(even, skip_e, skip_o)
    r_skip_ref[...] = jnp.where(even, g_e, g_o)
    l_mir_ref[...] = jnp.where(even, m0, m1)
    r_mir_ref[...] = jnp.where(even, q_o, q_e)


def enc_back_kernel(
    count, combine, core_ref, d_ref, high_ref, low_back_ref, x0_ref, low0_ref, x1_ref,
    slope0_ref, slope1_ref, stat_ref, members_ref,
    own_in, oth_in, own_out, oth_out,
    down_ref, r_out_ref, r_in_ref,
    w_in, w_out, sems,
):
    core = core_ref[0]
    loader = Loader(core, sems)
    out_ready = loader.pair(own_out, oth_out, w_out)
    in_ready = loader.pair(own_in, oth_in, w_in)
    members = members_ref[...]
    channels = x1_ref.shape[-1]

    t1 = d_ref[...].astype(F32)
    if not combine:
        t1 = t1 + high_ref[...].astype(F32)
    low_t1 = t1.astype(BF16)
    out_ready()
    e1 = (dot_t(low_t1, w_out[1]) * slope1_ref[...]).astype(BF16)
    in_ready()
    x1 = x1_ref[...].astype(F32).reshape(count, -1, channels)
    scale1 = stat_ref[3]
    normed1 = (x1 - stat_ref[2][:count][:, None, :]) * scale1[:count][:, None, :]
    back1 = norm_back(dot_t(e1, w_in[1]), normed1, scale1, members, count)
    d1 = (t1 + back1).astype(BF16)
    t0 = d1.astype(F32) + low_back_ref[...].astype(F32)
    low_t0 = t0.astype(BF16)
    e0 = (dot_t(low_t0, w_out[0]) * slope0_ref[...]).astype(BF16)
    if not combine:
        x0 = x0_ref[...].astype(F32).reshape(count, -1, channels)
        scale0 = stat_ref[1]
        normed0 = (x0 - stat_ref[0][:count][:, None, :]) * scale0[:count][:, None, :]
        back0 = norm_back(dot_t(e0, w_in[0]), normed0, scale0, members, count)
        down_ref[...] = (t0 + back0).astype(BF16)
    even = core == 0
    r_out_ref[...] = jnp.where(even, low_t0, low_t1)
    r_in_ref[...] = jnp.where(even, e0, e1)


def products_kernel(la_ref, ra_ref, lb_ref, rb_ref, a_ref, b_ref):
    a_ref[...] = dot_tn(la_ref[...], ra_ref[...]).astype(BF16)
    b_ref[...] = dot_tn(lb_ref[...], rb_ref[...]).astype(BF16)


VMEM = pl.BlockSpec(memory_space=pltpu.VMEM)
SMEM = pl.BlockSpec(memory_space=pltpu.SMEM)
ANY = pl.BlockSpec(memory_space=pl.ANY)


def pair_scratch(channels, pairs):
    return [pltpu.VMEM((2, channels, channels), BF16) for _ in range(pairs)] + [
        pltpu.SemaphoreType.DMA((2 * pairs,))
    ]


def estimate(rows, channels, products):
    return pl.CostEstimate(
        flops=2 * rows * channels * channels * products,
        bytes_accessed=2 * channels * channels * products,
        transcendentals=0,
    )


def enc_fwd(count, core, x, cond, members, w):
    rows, channels = x.shape
    low = jax.ShapeDtypeStruct((rows, channels), BF16)
    wide = jax.ShapeDtypeStruct((rows, channels), F32)
    stat = jax.ShapeDtypeStruct((4, cond.shape[0], channels), F32)
    tiny = jax.ShapeDtypeStruct((8, 128), BF16)
    return pl.pallas_call(
        functools.partial(enc_fwd_kernel, count),
        out_shape=(low, low, low, low, wide, wide, stat, tiny),
        in_specs=[SMEM] + [VMEM] * 3 + [ANY] * 4,
        out_specs=(VMEM,) * 8,
        scratch_shapes=pair_scratch(channels, 2),
        cost_estimate=estimate(rows, channels, 4),
        name="enc_fwd",
    )(core, x, cond, members, *w["in"], *w["out"])


def dec_both(count, combine, core, x, m0, m1, cond, d, members, w):
    rows, channels = x.shape
    low = jax.ShapeDtypeStruct((rows, channels), BF16)
    tiny = jax.ShapeDtypeStruct((8, 128), BF16)
    return pl.pallas_call(
        functools.partial(dec_kernel, count, combine),
        out_shape=(low, tiny if combine else low) + (low,) * 9,
        in_specs=[SMEM] + [VMEM] * 6 + [ANY] * 8,
        out_specs=(VMEM,) * 11,
        scratch_shapes=pair_scratch(channels, 4),
        cost_estimate=estimate(rows, channels, 15),
        name="dec_both",
    )(core, x, m0, m1, cond, d, members, *w["in"], *w["out"], *w["skip"], *w["mirror"])


def enc_back(count, combine, core, d, high, low_back, x0, x1, slopes, stat, members, w):
    rows, channels = x1.shape
    low = jax.ShapeDtypeStruct((rows, channels), BF16)
    tiny = jax.ShapeDtypeStruct((8, 128), BF16)
    return pl.pallas_call(
        functools.partial(enc_back_kernel, count, combine),
        out_shape=(tiny if combine else low, low, low),
        in_specs=[SMEM] + [VMEM] * 10 + [ANY] * 4,
        out_specs=(VMEM,) * 3,
        scratch_shapes=pair_scratch(channels, 2),
        cost_estimate=estimate(rows, channels, 4),
        name="enc_back",
    )(core, d, high, low_back, x0, x0, x1, *slopes, stat, members, *w["in"], *w["out"])


def products(la, ra, lb, rb):
    rows, channels = la.shape
    out = jax.ShapeDtypeStruct((channels, channels), BF16)
    return pl.pallas_call(
        products_kernel,
        out_shape=(out, out),
        in_specs=[VMEM] * 4,
        out_specs=(VMEM,) * 2,
        cost_estimate=estimate(rows, channels, 2),
        name="products",
    )(la, ra, lb, rb)


def swap_core(block):
    count = lax.axis_size("segment")
    return lax.ppermute(block, "segment", [(s, s ^ 1) for s in range(count)])


def mirror_chip(block):
    count = lax.axis_size("segment")
    chips = count // 2
    route = [(s, 2 * (chips - 1 - s // 2) + s % 2) for s in range(count)]
    return lax.ppermute(block, "segment", [pair for pair in route if pair[0] != pair[1]])


def next_chip(block, steps):
    count = lax.axis_size("segment")
    route = [(s, s + 2 * steps) for s in range(count) if 0 <= s + 2 * steps < count]
    return lax.ppermute(block, "segment", route)


def factors_of(size):
    found, rest, stride = [], size, 1
    while rest > 1:
        step = next(k for k in range(2, rest + 1) if rest % k == 0)
        found.append((stride, step))
        stride *= step
        rest //= step
    return found


def exchange(block, axis, stride, step, name):
    size = lax.axis_size(name)
    place = lax.axis_index(name) // stride % step
    total = lax.dynamic_index_in_dim(block, place, axis, keepdims=False).astype(F32)
    for offset in range(1, step):
        route = []
        for d in range(size):
            p = d // stride % step
            route.append((d, d + (((p + offset) % step) - p) * stride))
        sent = lax.dynamic_index_in_dim(block, (place + offset) % step, axis, keepdims=False)
        total = total + lax.ppermute(sent, name, route).astype(F32)
    return total


def halving(block, order, name):
    size = lax.axis_size(name)
    factors = factors_of(size)
    dims = [step for _, step in reversed(factors)]
    total = block.reshape(dims + [block.shape[0] // size] + list(block.shape[1:]))
    left = list(reversed(range(len(factors))))
    for which in order:
        stride, step = factors[which]
        axis = left.index(which)
        total = exchange(total.astype(block.dtype), axis, stride, step, name)
        left.remove(which)
    return total


def orders_of(size):
    count = len(factors_of(size))
    first = list(range(count))
    return first, first[1:] + first[:1]


def scatter_pair(first, second, name):
    order_a, order_b = orders_of(lax.axis_size(name))
    return halving(first, order_a, name), halving(second, order_b, name)


def time_embedding(steps, channels):
    half_width = channels // 2
    freqs = jnp.exp(-math.log(10000.0) * jnp.arange(half_width, dtype=F32) / half_width)
    angles = steps.astype(F32)[:, None] * freqs[None, :]
    return jnp.concatenate([jnp.cos(angles), jnp.sin(angles)], axis=-1)


def pooled_text(text_ids, text_table, micro_count):
    vocab_rows = text_table.shape[0]
    first_word = lax.axis_index(("dp", "segment")) * vocab_rows
    vocab_ids = first_word + lax.iota(jnp.int32, vocab_rows)
    counts = jnp.sum((text_ids[None, :, :] == vocab_ids[:, None, None]).astype(F32), axis=-1)
    partial = lax.dot_general(
        counts.astype(BF16), text_table, (((0,), (0,)), ((), ())), preferred_element_type=F32
    )
    partial = partial + swap_core(partial)
    size = lax.axis_size("dp")
    total = halving(partial, orders_of(size)[0], "dp")
    count = lax.axis_size("segment")
    stride = 2
    for _, step in factors_of(count // 2):
        part = total
        for offset in range(1, step):
            route = []
            for s in range(count):
                p = s // stride % step
                route.append((s, s + (((p + offset) % step) - p) * stride))
            total = total + lax.ppermute(part, "segment", route)
        stride *= step
    return total / text_ids.shape[1]


def keep(active, new, old):
    if old is None:
        return new
    return jax.tree.map(lambda n, o: jnp.where(active, n, o), new, old)


def dec_forward(count, x, m0, m1, cond, members, even, w):
    def sorted_pair(pair):
        own, other = pair
        return jnp.where(even, own, other), jnp.where(even, other, own)

    w_in, w_out, w_skip, w_mir = (sorted_pair(w[k]) for k in ("in", "out", "skip", "mirror"))
    for slot, source in ((0, m1), (1, m0)):
        skip = dot(source, w_mir[1 - slot]).astype(BF16)
        z = x.astype(F32) + dot(skip, w_skip[slot])
        low = as_low(norm(z, members, count)[0])
        hidden, _ = activate(block_pre_act(low, w_in[slot], cond, count))
        x = (z + dot(hidden, w_out[slot])).astype(BF16)
    return x


def on_device(
    features, timesteps, text_ids, text_table, in_weights, out_weights, skip_weights, cotangent
):
    segments = lax.axis_size("segment")
    chips = segments // 2
    half = chips // 2
    segment = lax.axis_index("segment")
    chip = segment // 2
    core = (segment % 2).astype(jnp.int32).reshape(1)
    is_dec = chip >= half
    channels = features.shape[-1]
    count = timesteps.shape[0]
    single = half == 1

    own_in, own_out, own_skip = in_weights[0], out_weights[0], skip_weights[0]
    own_mirror = mirror_chip(own_skip)
    w = {
        "in": (own_in, swap_core(own_in)),
        "out": (own_out, swap_core(own_out)),
        "skip": (own_skip, swap_core(own_skip)),
        "mirror": (own_mirror, swap_core(own_mirror)),
    }
    group = lax.iota(jnp.int32, channels) // (channels // GROUPS)
    members = (group[:, None] == group[None, :]).astype(BF16)

    cond = time_embedding(timesteps, channels) + pooled_text(text_ids, text_table, count)
    cond = jnp.pad(cond, ((0, -count % 8), (0, 0)))

    state, saved = features, None
    for j in range(half):
        x1, x2, hidden, low, slope0, slope1, stat, _ = enc_fwd(
            count, core, state, cond, members, w
        )
        saved = keep(chip == j, (state, x1, x2, hidden, low, slope0, slope1, stat), saved)
        if not single:
            state = next_chip(x2, 1)
    x0, x1, x2, enc_hidden, enc_low, slope0, slope1, stat = saved
    m0, m1 = mirror_chip(x1), mirror_chip(x2)
    if single:
        state = m1

    entry = None
    for j in range(half):
        entry = keep(chip == half + j, state, entry)
        if j < half - 1:
            state = next_chip(
                dec_forward(count, state, m0, m1, cond, members, core[0] == 0, w), 1
            )

    d_in, saved = cotangent, None
    for j in reversed(range(half)):
        outs = dec_both(count, single, core, entry, m0, m1, cond, d_in, members, w)
        saved = keep(chip == half + j, outs, saved)
        d_in = next_chip(outs[0], -1) if not single else mirror_chip(outs[0])
    _, high, low_back, l_out, r_out, l_in, r_in, l_skip, r_skip, l_mir, r_mir = saved
    low_back = mirror_chip(low_back)
    if not single:
        high = mirror_chip(high)
    skip_pair = products(l_skip, r_skip, l_mir, r_mir)
    own_skip_grad, mirror_skip_grad = scatter_pair(*skip_pair, "dp")
    mirror_skip_grad = mirror_chip(mirror_skip_grad)

    saved = None
    for j in reversed(range(half)):
        outs = enc_back(
            count, single, core, d_in, high, low_back, x0, x1, (slope0, slope1), stat, members, w
        )
        saved = keep(chip == j, outs, saved)
        if not single and j > 0:
            d_in = next_chip(outs[0], -1)
    _, enc_r_out, enc_r_in = saved

    pair = products(
        jnp.where(is_dec, l_out, enc_hidden),
        jnp.where(is_dec, r_out, enc_r_out),
        jnp.where(is_dec, l_in, enc_low),
        jnp.where(is_dec, r_in, enc_r_in),
    )
    grad_out, grad_in = scatter_pair(*pair, "dp")
    grad_skip = jnp.where(is_dec, own_skip_grad, mirror_skip_grad)
    return (grad_in[None], grad_out[None], grad_skip[None])


def solution(mesh):
    in_specs = (
        P("dp", None),
        P("dp"),
        P(),
        P(("dp", "segment"), None),
        P("segment", None, None),
        P("segment", None, None),
        P("segment", None, None),
        P("dp", None),
    )
    out_specs = (P("segment", "dp", None), P("segment", "dp", None), P("segment", "dp", None))
    return jax.shard_map(
        on_device, mesh=mesh, in_specs=in_specs, out_specs=out_specs, check_vma=False
    )
```

time: 517 us -> 123 us (0.24)
  waiting for transfers between devices: 219 us -> 44.3 us
  other arithmetic: 87.2 us -> 9.45 us
  blocking collectives: 42.6 us -> 0 us
  local copies, waits for them, and re-layouts: 43.7 us -> 4.88 us
  matrix products: 37 us -> 0.19 us
  starting transfers between devices: 70.7 us -> 34.8 us
  Pallas kernels: 0 us -> 28.2 us
  between operations: 13.9 us -> 1.04 us
    reduce_scatter x3 -> x0, waiting for transfers between devices: 174 us -> none  [the longest x1 59 us: on_device(): lax.psum_scatter(grad_sums[0].astype(jnp.bfloat16), 'dp', scatter_dimensi...]
    add x19 -> x7, other arithmetic: 61.7 us -> 0.15 us  [the longest x1 0.08 us: on_device(): time_embedding(timesteps, channels)]
    psum x1 -> x0, blocking collectives: 42.6 us -> none  [on_device(): pooled_all = lax.psum(partial_sum, ('dp', 'segment'))]
    dot_general x26 -> x1, matrix products: 37 us -> 0.19 us  [pooled_text(): lax.dot_general(counts.astype(BF16), text_table, (((0,), (0,)), ((), ()))...]
    ppermute x18 -> x27, starting transfers between devices: 70.6 us -> 34.8 us  [the longest x15 24 us: exchange(): total = total + lax.ppermute(sent, name, route).astype(F32)]
    broadcast_in_dim x70 -> x0, local copies, waits for them, and re-layouts: 31.6 us -> none  [the longest x15 19.8 us: on_device(): zero_matrix = jnp.zeros((channels, channels), jnp.float32)]
    pallas_call x0 -> x5, Pallas kernels: none -> 28.2 us  [the longest x1 10.7 us: dec_both(): pl.pallas_call(functools.partial(dec_kernel, count, combine), out_shape=(...]
    convert_element_type x6 -> x10, other arithmetic: 12.4 us -> 1.78 us  [the longest x1 1.11 us: on_device(): members = (group[:, None] == group[None, :]).astype(BF16)]
  transfers between devices with their start and end apart: 21 -> 27, of which waited for: 20 -> 16; matrix products, arithmetic and copies ran while one was open for 14% -> 8% of each run, Pallas kernels for 0% -> 14%
where the time goes in v1:
time: 123 us
  waiting for transfers between devices  44.3 us (36%)
  starting transfers between devices  34.8 us (28%)
  Pallas kernels  28.2 us (23%)
  other arithmetic  9.45 us (8%)
  local copies, waits for them, and re-layouts  4.88 us (4%)
    ppermute x15, starting transfers between devices, exchange(): total = total + lax.ppermute(sent, name, route).astype(F32)  24 us
    ppermute x15, waiting for transfers between devices, exchange(): total = total + lax.ppermute(sent, name, route).astype(F32)  21.8 us
    ppermute x6, waiting for transfers between devices, mirror_chip(): lax.ppermute(block, 'segment', [pair for pair in route if pair[0] != pair...  20.6 us
    pallas_call x1, Pallas kernels, dec_both(): pl.pallas_call(functools.partial(dec_kernel, count, combine), out_shape=(...  10.7 us
    ppermute x6, starting transfers between devices, mirror_chip(): lax.ppermute(block, 'segment', [pair for pair in route if pair[0] != pair...  7.72 us
    pallas_call x2, Pallas kernels, products(): pl.pallas_call(products_kernel, out_shape=(out, out), in_specs=[VMEM] * 4...  6.15 us
    pallas_call x1, Pallas kernels, enc_back(): pl.pallas_call(functools.partial(enc_back_kernel, count, combine), out_sh...  5.78 us
    pallas_call x1, Pallas kernels, enc_fwd(): pl.pallas_call(functools.partial(enc_fwd_kernel, count), out_shape=(low,...  5.61 us
  transfers between devices with their start and end apart: 27, of which 16 were waited for; matrix products, arithmetic and copies ran while one was open for 8% of the time, Pallas kernels for 14%

profile of v1, /device:TPU:0, one launch (start us, length us, event | category | flops | bytes accessed | tf_op | source)
XLA Modules:
  0.0 122.8 jit_solution(5452842872496965765)
XLA Ops:
  0.7 1.3 %convert_reduce_fusion = bf16[512,24]{0,1:T(8,128)(2,1)S(1)} fusion(s32[512]{0:T(512)S(1)} %iota_add_fusion, s32[24,64]{1,0:T(8,128)} %param.10), kind=kLoop, calls=%fused_computation | loop fusion | flops 2347008 | bytes 32768 | tf_op jit(solution)/shard_map/reduce_sum | solution.py:411
  2.0 0.2 fusion.17
  2.2 0.6 collective-permute-start
  2.8 2.6 %collective-permute-start.10 = (bf16[640,640]{1,0:T(8,128)(2,1)}, bf16[640,640]{1,0:T(8,128)(2,1)S(1)}, u32[]{:S(2)}, u32[]{:S(2)}) collective-permute-start(bf16[640,640]{1,0:T(8,128)(2,1)} %bitcast.120), channel_id=1, source_target_pairs={{0,2},{1,3},{2,0},{3,1},{4,6},{5,7},{6,4},{7,5},{8,10},{9,11},{10,... | collective-permute-start | bytes 2457608 | tf_op jit(solution)/shard_map/ppermute | solution.py:342
  5.3 0.2 collective-permute-start.9
  5.5 0.4 collective-permute-start.5
  5.8 0.2 collective-permute-start.6
  6.1 1.6 %collective-permute-start.1 = (f32[2,2,3,640]{3,1,2,0:T(2,128)S(1)}, f32[2,2,3,640]{3,1,2,0:T(2,128)S(1)}, u32[]{:S(2)}, u32[]{:S(2)}) collective-permute-start(f32[2,2,3,640]{3,1,2,0:T(2,128)S(1)} %bitcast.117), channel_id=1, source_target_pairs={{0,4},{4,0},{8,12},{12,8},{16,20},{20,16},{24,28},{28,24},{1,5},{5... | collective-permute-start | bytes 92168 | tf_op jit(solution)/shard_map/ppermute | solution.py:371
  7.7 2.4 %collective-permute-done.1 = f32[2,2,3,640]{3,1,2,0:T(2,128)S(1)} collective-permute-done((f32[2,2,3,640]{3,1,2,0:T(2,128)S(1)}, f32[2,2,3,640]{3,1,2,0:T(2,128)S(1)}, u32[]{:S(2)}, u32[]{:S(2)}) %collective-permute-start.1) | collective-permute-done | bytes 30752 | tf_op jit(solution)/shard_map/ppermute | solution.py:371
  10.2 1.6 %collective-permute-start.2 = (f32[2,3,640]{2,0,1:T(2,128)S(1)}, f32[2,3,640]{2,0,1:T(2,128)S(1)}, u32[]{:S(2)}, u32[]{:S(2)}) collective-permute-start(f32[2,3,640]{2,0,1:T(2,128)S(1)} %bitcast.118), channel_id=1, source_target_pairs={{0,8},{4,12},{8,0},{12,4},{16,24},{20,28},{24,16},{28,20},{1,9},{5... | collective-permute-start | bytes 46088 | tf_op jit(solution)/shard_map/ppermute | solution.py:371
  11.8 1.1 compare_convert_fusion.members_ref
  12.9 1.0 collective-permute-done.2
  14.0 2.7 %collective-permute-start.3 = (f32[3,640]{1,0:T(4,128)S(1)}, f32[3,640]{1,0:T(4,128)S(1)}, u32[]{:S(2)}, u32[]{:S(2)}) collective-permute-start(f32[3,640]{1,0:T(4,128)S(1)} %bitcast.119), channel_id=1, source_target_pairs={{0,16},{4,20},{8,24},{12,28},{16,0},{20,4},{24,8},{28,12},{1,17},{... | collective-permute-start | bytes 23048 | tf_op jit(solution)/shard_map/ppermute | solution.py:371
  16.7 7.7 %collective-permute-done.10.own_mir = bf16[640,640]{1,0:T(8,128)(2,1)S(1)} collective-permute-done((bf16[640,640]{1,0:T(8,128)(2,1)}, bf16[640,640]{1,0:T(8,128)(2,1)S(1)}, u32[]{:S(2)}, u32[]{:S(2)}) %collective-permute-start.10) | collective-permute-done | bytes 819232 | tf_op jit(solution)/shard_map/ppermute | solution.py:342
  24.4 1.8 %collective-permute-start.4 = (f32[3,640]{1,0:T(4,128)S(1)}, f32[3,640]{1,0:T(4,128)S(1)}, u32[]{:S(2)}, u32[]{:S(2)}) collective-permute-start(f32[3,640]{1,0:T(4,128)S(1)} %bitcast_add_fusion.2), channel_id=1, source_target_pairs={{0,2},{1,3},{2,0},{3,1},{4,6},{5,7},{6,4},{7,5},{8,10},{9,11},{10,... | collective-permute-start | bytes 23048 | tf_op jit(solution)/shard_map/ppermute | solution.py:427
  26.4 1.8 %collective-permute-done.4 = f32[3,640]{1,0:T(4,128)S(1)} collective-permute-done((f32[3,640]{1,0:T(4,128)S(1)}, f32[3,640]{1,0:T(4,128)S(1)}, u32[]{:S(2)}, u32[]{:S(2)}) %collective-permute-start.4) | collective-permute-done | bytes 7712 | tf_op jit(solution)/shard_map/ppermute | solution.py:427
  28.2 0.6 pad.4.cond_ref
  28.9 0.9 copy-done.1
  29.7 0.3 copy-done.2
  30.0 5.6 %enc_fwd.1 = (bf16[192,640]{1,0:T(8,128)(2,1)}, bf16[192,640]{1,0:T(8,128)(2,1)}, bf16[192,640]{1,0:T(8,128)(2,1)}, bf16[192,640]{1,0:T(8,128)(2,1)}, f32[192,64...) custom-call(s32[1]{0:T(128)} %bitcast.core_ref, bf16[192,640]{1,0:T(8,128)(2,1)} %low0_ref.1, ...), custom_call_target="tpu_custom_call" | custom-call | flops 629145600 | bytes 3276800 | tf_op jit(solution)/shard_map/enc_fwd/pallas_call | solution.py:279
  35.6 1.8 %collective-permute-start.7 = (bf16[192,640]{1,0:T(8,128)(2,1)}, bf16[192,640]{1,0:T(8,128)(2,1)S(1)}, u32[]{:S(2)}, u32[]{:S(2)}) collective-permute-start(bf16[192,640]{1,0:T(8,128)(2,1)} %get-tuple-element.27), channel_id=1, source_target_pairs={{0,2},{1,3},{2,0},{3,1},{4,6},{5,7},{6,4},{7,5},{8,10},{9,11},{10,... | collective-permute-start | bytes 737288 | tf_op jit(solution)/shard_map/ppermute | solution.py:342
  37.4 0.3 collective-permute-start.8
  37.7 7.0 %collective-permute-done.7.x_ref.m1_ref = bf16[192,640]{1,0:T(8,128)(2,1)S(1)} collective-permute-done((bf16[192,640]{1,0:T(8,128)(2,1)}, bf16[192,640]{1,0:T(8,128)(2,1)S(1)}, u32[]{:S(2)}, u32[]{:S(2)}) %collective-permute-start.7) | collective-permute-done | bytes 245792 | tf_op jit(solution)/shard_map/ppermute | solution.py:342
  44.7 3.7 %collective-permute-done.8.m0_ref = bf16[192,640]{1,0:T(8,128)(2,1)S(1)} collective-permute-done((bf16[192,640]{1,0:T(8,128)(2,1)}, bf16[192,640]{1,0:T(8,128)(2,1)S(1)}, u32[]{:S(2)}, u32[]{:S(2)}) %collective-permute-start.8) | collective-permute-done | bytes 245792 | tf_op jit(solution)/shard_map/ppermute | solution.py:342
  48.4 0.7 copy-done.18
  49.1 10.7 %dec_both.1 = (bf16[192,640]{1,0:T(8,128)(2,1)}, bf16[8,128]{1,0:T(8,128)(2,1)}, bf16[192,640]{1,0:T(8,128)(2,1)}, bf16[192,640]{1,0:T(8,128)(2,1)}, bf16[192,64...) custom-call(s32[1]{0:T(128)} %bitcast.core_ref, ...), custom_call_target="tpu_custom_call" | custom-call | flops 2359296000 | bytes 12288000 | tf_op jit(solution)/shard_map/dec_both/pallas_call | solution.py:294
  59.8 1.8 %collective-permute-start.12 = (bf16[192,640]{1,0:T(8,128)(2,1)}, bf16[192,640]{1,0:T(8,128)(2,1)S(1)}, u32[]{:S(2)}, u32[]{:S(2)}) collective-permute-start(bf16[192,640]{1,0:T(8,128)(2,1)} %get-tuple-element.32), channel_id=1, source_target_pairs={{0,2},{1,3},{2,0},{3,1},{4,6},{5,7},{6,4},{7,5},{8,10},{9,11},{10,... | collective-permute-start | bytes 737288 | tf_op jit(solution)/shard_map/ppermute | solution.py:342
  61.6 0.3 collective-permute-start.13
  61.9 3.1 %products.3 = (bf16[640,640]{1,0:T(8,128)(2,1)}, bf16[640,640]{1,0:T(8,128)(2,1)}) custom-call(bf16[192,640]{1,0:T(8,128)(2,1)} %get-tuple-element.45.la_ref, bf16[192,640]{1,0:T(8,128)(2,1)} %get-tuple-element.46.ra_ref, bf16[192,640]{1,0:T(8,128)(2,1)} %get-tuple-element.47.lb_ref, bf16[192,640]{1,0:T(8,128)(2,1)} %get-tuple-element.48.rb_ref), custom_call_target="tpu_custom_call" | custom-call | flops 314572800 | bytes 1638400 | tf_op jit(solution)/shard_map/products/pallas_call | solution.py:323
  64.9 1.1 dynamic-slice_bitcast_fusion
  66.0 1.9 %collective-permute-start.23 = (bf16[2,2,80,640]{3,2,1,0:T(8,128)(2,1)S(1)}, bf16[2,2,80,640]{3,2,1,0:T(8,128)(2,1)S(1)}, u32[]{:S(2)}, u32[]{:S(2)}) collective-permute-start(bf16[2,2,80,640]{3,2,1,0:T(8,128)(2,1)S(1)} %dynamic-slice_bitcast_fusion), channel_id=1, source_target_pairs={{0,8},{4,12},{8,0},{12,4},{16,24},{20,28},{24,16},{28,20},{1,9},{5... | collective-permute-start | bytes 1228808 | tf_op jit(solution)/shard_map/ppermute | solution.py:371
  67.9 0.7 broadcast_select_fusion.1.lb_ref
  68.7 0.7 broadcast_select_fusion.3.la_ref
  69.4 2.3 %collective-permute-done.13.low_back_ref = bf16[192,640]{1,0:T(8,128)(2,1)S(1)} collective-permute-done((bf16[192,640]{1,0:T(8,128)(2,1)}, bf16[192,640]{1,0:T(8,128)(2,1)S(1)}, u32[]{:S(2)}, u32[]{:S(2)}) %collective-permute-start.13) | collective-permute-done | bytes 245792 | tf_op jit(solution)/shard_map/ppermute | solution.py:342
  71.7 0.7 copy-done.12
  72.4 5.8 %enc_back.1 = (bf16[8,128]{1,0:T(8,128)(2,1)}, bf16[192,640]{1,0:T(8,128)(2,1)}, bf16[192,640]{1,0:T(8,128)(2,1)}) custom-call(s32[1]{0:T(128)} %bitcast.core_ref, bf16[192,640]{1,0:T(8,128)(2,1)} %copy-done.11, bf16[8,128]{1,0:T(8,128)(2,1)} %get-tuple-element.33.high_ref, bf16[192,640]{1,0:T(8,128)(2,1)} %copy-done.12, bf16[192,640]{1,0:T(8,128)(2,1)} %low0_ref.1, ...), custom_call_target="tpu_custom_call" | custom-call | flops 629145600 | bytes 3276800 | tf_op jit(solution)/shard_map/enc_back/pallas_call | solution.py:309
  78.2 1.7 %broadcast_select_fusion.2.ra_ref = bf16[192,640]{1,0:T(8,128)(2,1)} fusion(bf16[192,640]{1,0:T(8,128)(2,1)S(1)} %copy-done.10, bf16[192,640]{1,0:T(8,128)(2,1)} %get-tuple-element.38, pred[]{:T(512)S(6)} %ge.3), kind=kLoop, calls=%fused_computation.26 | loop fusion | flops 122880 | bytes 737281 | tf_op jit(solution)/shard_map/jit(_where)/select_n | solution.py:527
  79.9 0.7 broadcast_select_fusion.rb_ref
  80.7 3.1 %products.2 = (bf16[640,640]{1,0:T(8,128)(2,1)}, bf16[640,640]{1,0:T(8,128)(2,1)}) custom-call(bf16[192,640]{1,0:T(8,128)(2,1)} %broadcast_select_fusion.3.la_ref, bf16[192,640]{1,0:T(8,128)(2,1)} %broadcast_select_fusion.2.ra_ref, bf16[192,640]{1,0:T(8,128)(2,1)} %broadcast_select_fusion.1.lb_ref, bf16[192,640]{1,0:T(8,128)(2,1)} %broadcast_select_fusion.rb_ref), custom_call_target="tpu_custom_call" | custom-call | flops 314572800 | bytes 1638400 | tf_op jit(solution)/shard_map/products/pallas_call | solution.py:323
  83.9 2.9 %collective-permute-start.24 = (bf16[2,80,640]{2,1,0:T(8,128)(2,1)S(1)}, bf16[2,80,640]{2,1,0:T(8,128)(2,1)S(1)}, u32[]{:S(2)}, u32[]{:S(2)}) collective-permute-start(bf16[2,80,640]{2,1,0:T(8,128)(2,1)S(1)} %dynamic-slice_bitcast_fusion.2), channel_id=1, source_target_pairs={{0,16},{4,20},{8,24},{12,28},{16,0},{20,4},{24,8},{28,12},{1,17},{... | collective-permute-start | bytes 614408 | tf_op jit(solution)/shard_map/ppermute | solution.py:371
  86.8 1.7 %collective-permute-start.14 = (bf16[2,2,80,640]{3,2,1,0:T(8,128)(2,1)S(1)}, bf16[2,2,80,640]{3,2,1,0:T(8,128)(2,1)S(1)}, u32[]{:S(2)}, u32[]{:S(2)}) collective-permute-start(bf16[2,2,80,640]{3,2,1,0:T(8,128)(2,1)S(1)} %dynamic-slice_bitcast_fusion.1), channel_id=1, source_target_pairs={{0,8},{4,12},{8,0},{12,4},{16,24},{20,28},{24,16},{28,20},{1,9},{5... | collective-permute-start | bytes 1228808 | tf_op jit(solution)/shard_map/ppermute | solution.py:371
  88.5 0.1 constant_dynamic-slice_fusion.1
  88.7 1.6 %collective-permute-start.17 = (bf16[2,2,80,640]{3,2,0,1:T(8,128)(2,1)S(1)}, bf16[2,2,80,640]{3,2,0,1:T(8,128)(2,1)S(1)}, u32[]{:S(2)}, u32[]{:S(2)}) collective-permute-start(bf16[2,2,80,640]{3,2,0,1:T(8,128)(2,1)S(1)} %bitcast.116), channel_id=1, source_target_pairs={{0,4},{4,0},{8,12},{12,8},{16,20},{20,16},{24,28},{28,24},{1,5},{5... | collective-permute-start | bytes 1228808 | tf_op jit(solution)/shard_map/ppermute | solution.py:371
  90.3 0.5 collective-permute-start.20
  90.8 3.3 %collective-permute-done.24 = bf16[2,80,640]{2,1,0:T(8,128)(2,1)S(1)} collective-permute-done((bf16[2,80,640]{2,1,0:T(8,128)(2,1)S(1)}, bf16[2,80,640]{2,1,0:T(8,128)(2,1)S(1)}, u32[]{:S(2)}, u32[]{:S(2)}) %collective-permute-start.24) | collective-permute-done | bytes 204832 | tf_op jit(solution)/shard_map/ppermute | solution.py:371
  94.2 1.6 %collective-permute-start.25 = (bf16[80,640]{1,0:T(8,128)(2,1)S(1)}, bf16[80,640]{1,0:T(8,128)(2,1)S(1)}, u32[]{:S(2)}, u32[]{:S(2)}) collective-permute-start(bf16[80,640]{1,0:T(8,128)(2,1)S(1)} %dynamic-slice_bitcast_fusion.6), channel_id=1, source_target_pairs={{0,4},{4,0},{8,12},{12,8},{16,20},{20,16},{24,28},{28,24},{1,5},{5... | collective-permute-start | bytes 307208 | tf_op jit(solution)/shard_map/ppermute | solution.py:371
  95.8 3.0 %collective-permute-done.14 = bf16[2,2,80,640]{3,2,1,0:T(8,128)(2,1)S(1)} collective-permute-done((bf16[2,2,80,640]{3,2,1,0:T(8,128)(2,1)S(1)}, bf16[2,2,80,640]{3,2,1,0:T(8,128)(2,1)S(1)}, u32[]{:S(2)}, u32[]{:S(2)}) %collective-permute-start.14) | collective-permute-done | bytes 409632 | tf_op jit(solution)/shard_map/ppermute | solution.py:371
  99.0 1.5 %collective-permute-start.15 = (bf16[2,80,640]{2,1,0:T(8,128)(2,1)S(1)}, bf16[2,80,640]{2,1,0:T(8,128)(2,1)S(1)}, u32[]{:S(2)}, u32[]{:S(2)}) collective-permute-start(bf16[2,80,640]{2,1,0:T(8,128)(2,1)S(1)} %dynamic-slice_bitcast_fusion.5), channel_id=1, source_target_pairs={{0,16},{4,20},{8,24},{12,28},{16,0},{20,4},{24,8},{28,12},{1,17},{... | collective-permute-start | bytes 614408 | tf_op jit(solution)/shard_map/ppermute | solution.py:371
  100.5 0.6 collective-permute-done.17
  101.3 1.9 %collective-permute-start.18 = (bf16[2,80,640]{2,1,0:T(8,128)(2,1)S(1)}, bf16[2,80,640]{2,1,0:T(8,128)(2,1)S(1)}, u32[]{:S(2)}, u32[]{:S(2)}) collective-permute-start(bf16[2,80,640]{2,1,0:T(8,128)(2,1)S(1)} %dynamic-slice_bitcast_fusion.4), channel_id=1, source_target_pairs={{0,8},{4,12},{8,0},{12,4},{16,24},{20,28},{24,16},{28,20},{1,9},{5... | collective-permute-start | bytes 614408 | tf_op jit(solution)/shard_map/ppermute | solution.py:371
  103.2 3.9 %collective-permute-done.20 = bf16[2,2,80,640]{3,2,0,1:T(8,128)(2,1)S(1)} collective-permute-done((bf16[2,2,80,640]{3,2,0,1:T(8,128)(2,1)S(1)}, bf16[2,2,80,640]{3,2,0,1:T(8,128)(2,1)S(1)}, u32[]{:S(2)}, u32[]{:S(2)}) %collective-permute-start.20) | collective-permute-done | bytes 409632 | tf_op jit(solution)/shard_map/ppermute | solution.py:371
  107.2 0.5 collective-permute-start.21
  107.7 0.5 collective-permute-done.25
  108.2 1.0 collective-permute-start.26
  109.3 1.6 %collective-permute-start.16 = (bf16[80,640]{1,0:T(8,128)(2,1)S(1)}, bf16[80,640]{1,0:T(8,128)(2,1)S(1)}, u32[]{:S(2)}, u32[]{:S(2)}) collective-permute-start(bf16[80,640]{1,0:T(8,128)(2,1)S(1)} %dynamic-slice_bitcast_fusion.9), channel_id=1, source_target_pairs={{0,4},{4,0},{8,12},{12,8},{16,20},{20,16},{24,28},{28,24},{1,5},{5... | collective-permute-start | bytes 307208 | tf_op jit(solution)/shard_map/ppermute | solution.py:371
  110.9 0.8 collective-permute-done.18
  111.7 1.2 collective-permute-start.19
  113.0 1.9 %collective-permute-done.21 = bf16[2,80,640]{2,1,0:T(8,128)(2,1)S(1)} collective-permute-done((bf16[2,80,640]{2,1,0:T(8,128)(2,1)S(1)}, bf16[2,80,640]{2,1,0:T(8,128)(2,1)S(1)}, u32[]{:S(2)}, u32[]{:S(2)}) %collective-permute-start.21) | collective-permute-done | bytes 204832 | tf_op jit(solution)/shard_map/ppermute | solution.py:371
  114.9 1.4 %collective-permute-start.22 = (bf16[80,640]{1,0:T(8,128)(2,1)S(1)}, bf16[80,640]{1,0:T(8,128)(2,1)S(1)}, u32[]{:S(2)}, u32[]{:S(2)}) collective-permute-start(bf16[80,640]{1,0:T(8,128)(2,1)S(1)} %dynamic-slice_bitcast_fusion.7), channel_id=1, source_target_pairs={{0,16},{4,20},{8,24},{12,28},{16,0},{20,4},{24,8},{28,12},{1,17},{... | collective-permute-start | bytes 307208 | tf_op jit(solution)/shard_map/ppermute | solution.py:371
  116.3 0.7 fusion.11
  117.0 2.9 %collective-permute-done.19 = bf16[80,640]{1,0:T(8,128)(2,1)S(1)} collective-permute-done((bf16[80,640]{1,0:T(8,128)(2,1)S(1)}, bf16[80,640]{1,0:T(8,128)(2,1)S(1)}, u32[]{:S(2)}, u32[]{:S(2)}) %collective-permute-start.19) | collective-permute-done | bytes 102432 | tf_op jit(solution)/shard_map/ppermute | solution.py:371
  119.9 0.7 fusion.10
  120.6 1.5 %collective-permute-done.22 = bf16[80,640]{1,0:T(8,128)(2,1)S(1)} collective-permute-done((bf16[80,640]{1,0:T(8,128)(2,1)S(1)}, bf16[80,640]{1,0:T(8,128)(2,1)S(1)}, u32[]{:S(2)}, u32[]{:S(2)}) %collective-permute-start.22) | collective-permute-done | bytes 102432 | tf_op jit(solution)/shard_map/ppermute | solution.py:371
  122.1 0.7 fusion.9
  (85 shorter events, 1.5 us)
Async XLA Ops:
  0.6 1.4 %copy-start = (bf16[512,640]{1,0:T(8,128)(2,1)S(1)}, bf16[512,640]{1,0:T(8,128)(2,1)}, u32[]{:S(2)}) copy-start(bf16[512,640]{1,0:T(8,128)(2,1)} %param.11) | copy-start | bytes 1966084
  2.2 3.8 %collective-permute-start = (f32[24,640]{1,0:T(8,128)S(1)}, f32[24,640]{1,0:T(8,128)S(1)}, u32[]{:S(2)}, u32[]{:S(2)}) collective-permute-start(f32[24,640]{1,0:T(8,128)S(1)} %fusion.17), channel_id=1, source_target_pairs={{0,1},{1,0},{2,3},{3,2},{4,5},{5,4},{6,7},{7,6},{8,9},{9,8},{10,11... | collective-permute-start | bytes 184328 | tf_op jit(solution)/shard_map/ppermute | solution.py:335
  2.8 21.6 %collective-permute-start.10 = (bf16[640,640]{1,0:T(8,128)(2,1)}, bf16[640,640]{1,0:T(8,128)(2,1)S(1)}, u32[]{:S(2)}, u32[]{:S(2)}) collective-permute-start(bf16[640,640]{1,0:T(8,128)(2,1)} %bitcast.120), channel_id=1, source_target_pairs={{0,2},{1,3},{2,0},{3,1},{4,6},{5,7},{6,4},{7,5},{8,10},{9,11},{10,... | collective-permute-start | bytes 2457608 | tf_op jit(solution)/shard_map/ppermute | solution.py:342
  5.3 32.4 %collective-permute-start.9 = (bf16[640,640]{1,0:T(8,128)(2,1)}, bf16[640,640]{1,0:T(8,128)(2,1)}, u32[]{:S(2)}, u32[]{:S(2)}) collective-permute-start(bf16[640,640]{1,0:T(8,128)(2,1)} %bitcast.121), channel_id=1, source_target_pairs={{0,1},{1,0},{2,3},{3,2},{4,5},{5,4},{6,7},{7,6},{8,9},{9,8},{10,11... | collective-permute-start | bytes 2457608 | tf_op jit(solution)/shard_map/ppermute | solution.py:335
  5.5 23.4 %collective-permute-start.5 = (bf16[640,640]{1,0:T(8,128)(2,1)}, bf16[640,640]{1,0:T(8,128)(2,1)S(1)}, u32[]{:S(2)}, u32[]{:S(2)}) collective-permute-start(bf16[640,640]{1,0:T(8,128)(2,1)} %bitcast.101), channel_id=1, source_target_pairs={{0,1},{1,0},{2,3},{3,2},{4,5},{5,4},{6,7},{7,6},{8,9},{9,8},{10,11... | collective-permute-start | bytes 2457608 | tf_op jit(solution)/shard_map/ppermute | solution.py:335
  5.8 23.0 %collective-permute-start.6 = (bf16[640,640]{1,0:T(8,128)(2,1)}, bf16[640,640]{1,0:T(8,128)(2,1)S(1)}, u32[]{:S(2)}, u32[]{:S(2)}) collective-permute-start(bf16[640,640]{1,0:T(8,128)(2,1)} %bitcast.105), channel_id=1, source_target_pairs={{0,1},{1,0},{2,3},{3,2},{4,5},{5,4},{6,7},{7,6},{8,9},{9,8},{10,11... | collective-permute-start | bytes 2457608 | tf_op jit(solution)/shard_map/ppermute | solution.py:335
  6.0 10.7 %copy-start.19 = (s32[3]{0:T(128)S(1)}, s32[3]{0:T(128)}, u32[]{:S(2)}) copy-start(s32[3]{0:T(128)} %param.9) | copy-start | bytes 40
  6.1 4.0 %collective-permute-start.1 = (f32[2,2,3,640]{3,1,2,0:T(2,128)S(1)}, f32[2,2,3,640]{3,1,2,0:T(2,128)S(1)}, u32[]{:S(2)}, u32[]{:S(2)}) collective-permute-start(f32[2,2,3,640]{3,1,2,0:T(2,128)S(1)} %bitcast.117), channel_id=1, source_target_pairs={{0,4},{4,0},{8,12},{12,8},{16,20},{20,16},{24,28},{28,24},{1,5},{5... | collective-permute-start | bytes 92168 | tf_op jit(solution)/shard_map/ppermute | solution.py:371
  10.2 3.8 %collective-permute-start.2 = (f32[2,3,640]{2,0,1:T(2,128)S(1)}, f32[2,3,640]{2,0,1:T(2,128)S(1)}, u32[]{:S(2)}, u32[]{:S(2)}) collective-permute-start(f32[2,3,640]{2,0,1:T(2,128)S(1)} %bitcast.118), channel_id=1, source_target_pairs={{0,8},{4,12},{8,0},{12,4},{16,24},{20,28},{24,16},{28,20},{1,9},{5... | collective-permute-start | bytes 46088 | tf_op jit(solution)/shard_map/ppermute | solution.py:371
  14.0 10.4 %collective-permute-start.3 = (f32[3,640]{1,0:T(4,128)S(1)}, f32[3,640]{1,0:T(4,128)S(1)}, u32[]{:S(2)}, u32[]{:S(2)}) collective-permute-start(f32[3,640]{1,0:T(4,128)S(1)} %bitcast.119), channel_id=1, source_target_pairs={{0,16},{4,20},{8,24},{12,28},{16,0},{20,4},{24,8},{28,12},{1,17},{... | collective-permute-start | bytes 23048 | tf_op jit(solution)/shard_map/ppermute | solution.py:371
  24.4 24.0 %copy-start.16 = (bf16[640,640]{1,0:T(8,128)(2,1)}, bf16[640,640]{1,0:T(8,128)(2,1)S(1)}, u32[]{:S(2)}) copy-start(bf16[640,640]{1,0:T(8,128)(2,1)S(1)} %collective-permute-done.10.own_mir) | copy-start | bytes 2457604
  24.4 24.0 %collective-permute-start.11 = (bf16[640,640]{1,0:T(8,128)(2,1)S(1)}, bf16[640,640]{1,0:T(8,128)(2,1)}, u32[]{:S(2)}, u32[]{:S(2)}) collective-permute-start(bf16[640,640]{1,0:T(8,128)(2,1)S(1)} %collective-permute-done.10.own_mir), channel_id=1, source_target_pairs={{0,1},{1,0},{2,3},{3,2},{4,5},{5,4},{6,7},{7,6},{8,9},{9,8},{10,11... | collective-permute-start | bytes 2457608 | tf_op jit(solution)/shard_map/ppermute | solution.py:335
  24.4 3.7 %collective-permute-start.4 = (f32[3,640]{1,0:T(4,128)S(1)}, f32[3,640]{1,0:T(4,128)S(1)}, u32[]{:S(2)}, u32[]{:S(2)}) collective-permute-start(f32[3,640]{1,0:T(4,128)S(1)} %bitcast_add_fusion.2), channel_id=1, source_target_pairs={{0,2},{1,3},{2,0},{3,1},{4,6},{5,7},{6,4},{7,5},{8,10},{9,11},{10,... | collective-permute-start | bytes 23048 | tf_op jit(solution)/shard_map/ppermute | solution.py:427
  28.8 0.9 copy-start.1
  28.8 1.2 copy-start.2
  35.6 9.1 %collective-permute-start.7 = (bf16[192,640]{1,0:T(8,128)(2,1)}, bf16[192,640]{1,0:T(8,128)(2,1)S(1)}, u32[]{:S(2)}, u32[]{:S(2)}) collective-permute-start(bf16[192,640]{1,0:T(8,128)(2,1)} %get-tuple-element.27), channel_id=1, source_target_pairs={{0,2},{1,3},{2,0},{3,1},{4,6},{5,7},{6,4},{7,5},{8,10},{9,11},{10,... | collective-permute-start | bytes 737288 | tf_op jit(solution)/shard_map/ppermute | solution.py:342
  37.4 10.9 %collective-permute-start.8 = (bf16[192,640]{1,0:T(8,128)(2,1)}, bf16[192,640]{1,0:T(8,128)(2,1)S(1)}, u32[]{:S(2)}, u32[]{:S(2)}) collective-permute-start(bf16[192,640]{1,0:T(8,128)(2,1)} %get-tuple-element.28.x1_ref), channel_id=1, source_target_pairs={{0,2},{1,3},{2,0},{3,1},{4,6},{5,7},{6,4},{7,5},{8,10},{9,11},{10,... | collective-permute-start | bytes 737288 | tf_op jit(solution)/shard_map/ppermute | solution.py:342
  44.7 3.7 %copy-start.17 = (bf16[192,640]{1,0:T(8,128)(2,1)}, bf16[192,640]{1,0:T(8,128)(2,1)S(1)}, u32[]{:S(2)}) copy-start(bf16[192,640]{1,0:T(8,128)(2,1)S(1)} %collective-permute-done.7.x_ref.m1_ref) | copy-start | bytes 737284
  48.4 0.7 copy-start.18
  59.8 9.6 %collective-permute-start.12 = (bf16[192,640]{1,0:T(8,128)(2,1)}, bf16[192,640]{1,0:T(8,128)(2,1)S(1)}, u32[]{:S(2)}, u32[]{:S(2)}) collective-permute-start(bf16[192,640]{1,0:T(8,128)(2,1)} %get-tuple-element.32), channel_id=1, source_target_pairs={{0,2},{1,3},{2,0},{3,1},{4,6},{5,7},{6,4},{7,5},{8,10},{9,11},{10,... | collective-permute-start | bytes 737288 | tf_op jit(solution)/shard_map/ppermute | solution.py:342
  61.6 10.1 %collective-permute-start.13 = (bf16[192,640]{1,0:T(8,128)(2,1)}, bf16[192,640]{1,0:T(8,128)(2,1)S(1)}, u32[]{:S(2)}, u32[]{:S(2)}) collective-permute-start(bf16[192,640]{1,0:T(8,128)(2,1)} %get-tuple-element.34), channel_id=1, source_target_pairs={{0,2},{1,3},{2,0},{3,1},{4,6},{5,7},{6,4},{7,5},{8,10},{9,11},{10,... | collective-permute-start | bytes 737288 | tf_op jit(solution)/shard_map/ppermute | solution.py:342
  61.9 6.0 %copy-start.8 = (bf16[192,640]{1,0:T(8,128)(2,1)S(1)}, bf16[192,640]{1,0:T(8,128)(2,1)}, u32[]{:S(2)}) copy-start(bf16[192,640]{1,0:T(8,128)(2,1)} %get-tuple-element.40) | copy-start | bytes 737284
  61.9 6.0 %copy-start.14 = (bf16[192,640]{1,0:T(8,128)(2,1)S(1)}, bf16[192,640]{1,0:T(8,128)(2,1)}, u32[]{:S(2)}) copy-start(bf16[192,640]{1,0:T(8,128)(2,1)} %get-tuple-element.39) | copy-start | bytes 737284
  64.9 3.7 %copy-start.7 = (bf16[192,640]{1,0:T(8,128)(2,1)S(1)}, bf16[192,640]{1,0:T(8,128)(2,1)}, u32[]{:S(2)}) copy-start(bf16[192,640]{1,0:T(8,128)(2,1)} %get-tuple-element.30) | copy-start | bytes 737284
  64.9 3.7 %copy-start.13 = (bf16[192,640]{1,0:T(8,128)(2,1)S(1)}, bf16[192,640]{1,0:T(8,128)(2,1)}, u32[]{:S(2)}) copy-start(bf16[192,640]{1,0:T(8,128)(2,1)} %get-tuple-element.29) | copy-start | bytes 737284
  66.0 17.7 %collective-permute-start.23 = (bf16[2,2,80,640]{3,2,1,0:T(8,128)(2,1)S(1)}, bf16[2,2,80,640]{3,2,1,0:T(8,128)(2,1)S(1)}, u32[]{:S(2)}, u32[]{:S(2)}) collective-permute-start(bf16[2,2,80,640]{3,2,1,0:T(8,128)(2,1)S(1)} %dynamic-slice_bitcast_fusion), channel_id=1, source_target_pairs={{0,8},{4,12},{8,0},{12,4},{16,24},{20,28},{24,16},{28,20},{1,9},{5... | collective-permute-start | bytes 1228808 | tf_op jit(solution)/shard_map/ppermute | solution.py:371
  69.4 2.3 %copy-start.11 = (bf16[192,640]{1,0:T(8,128)(2,1)}, bf16[192,640]{1,0:T(8,128)(2,1)S(1)}, u32[]{:S(2)}) copy-start(bf16[192,640]{1,0:T(8,128)(2,1)S(1)} %collective-permute-done.12.d_ref) | copy-start | bytes 737284
  71.7 0.7 copy-start.12
  72.4 5.8 %copy-start.10 = (bf16[192,640]{1,0:T(8,128)(2,1)S(1)}, bf16[192,640]{1,0:T(8,128)(2,1)}, u32[]{:S(2)}) copy-start(bf16[192,640]{1,0:T(8,128)(2,1)} %get-tuple-element.31) | copy-start | bytes 737284
  78.1 1.8 %copy-start.9 = (bf16[192,640]{1,0:T(8,128)(2,1)S(1)}, bf16[192,640]{1,0:T(8,128)(2,1)}, u32[]{:S(2)}) copy-start(bf16[192,640]{1,0:T(8,128)(2,1)} %get-tuple-element.41) | copy-start | bytes 737284
  78.2 1.8 %copy-start.15 = (bf16[192,640]{1,0:T(8,128)(2,1)S(1)}, bf16[192,640]{1,0:T(8,128)(2,1)}, u32[]{:S(2)}) copy-start(bf16[192,640]{1,0:T(8,128)(2,1)} %get-tuple-element.42) | copy-start | bytes 737284
  79.9 3.8 %copy-start.5 = (bf16[640,640]{1,0:T(8,128)(2,1)S(1)}, bf16[640,640]{1,0:T(8,128)(2,1)}, u32[]{:S(2)}) copy-start(bf16[640,640]{1,0:T(8,128)(2,1)} %get-tuple-element.50) | copy-start | bytes 2457604
  83.7 3.0 %copy-start.6 = (bf16[640,640]{1,0:T(8,128)(2,1)S(1)}, bf16[640,640]{1,0:T(8,128)(2,1)}, u32[]{:S(2)}) copy-start(bf16[640,640]{1,0:T(8,128)(2,1)} %get-tuple-element.43) | copy-start | bytes 2457604
  83.7 4.7 %copy-start.4 = (bf16[640,640]{1,0:T(8,128)(2,1)S(1)}, bf16[640,640]{1,0:T(8,128)(2,1)}, u32[]{:S(2)}) copy-start(bf16[640,640]{1,0:T(8,128)(2,1)} %get-tuple-element.44) | copy-start | bytes 2457604
  83.9 4.6 %copy-start.3 = (bf16[640,640]{1,0:T(8,128)(2,1)S(1)}, bf16[640,640]{1,0:T(8,128)(2,1)}, u32[]{:S(2)}) copy-start(bf16[640,640]{1,0:T(8,128)(2,1)} %get-tuple-element.49) | copy-start | bytes 2457604
  83.9 10.2 %collective-permute-start.24 = (bf16[2,80,640]{2,1,0:T(8,128)(2,1)S(1)}, bf16[2,80,640]{2,1,0:T(8,128)(2,1)S(1)}, u32[]{:S(2)}, u32[]{:S(2)}) collective-permute-start(bf16[2,80,640]{2,1,0:T(8,128)(2,1)S(1)} %dynamic-slice_bitcast_fusion.2), channel_id=1, source_target_pairs={{0,16},{4,20},{8,24},{12,28},{16,0},{20,4},{24,8},{28,12},{1,17},{... | collective-permute-start | bytes 614408 | tf_op jit(solution)/shard_map/ppermute | solution.py:371
  86.8 12.0 %collective-permute-start.14 = (bf16[2,2,80,640]{3,2,1,0:T(8,128)(2,1)S(1)}, bf16[2,2,80,640]{3,2,1,0:T(8,128)(2,1)S(1)}, u32[]{:S(2)}, u32[]{:S(2)}) collective-permute-start(bf16[2,2,80,640]{3,2,1,0:T(8,128)(2,1)S(1)} %dynamic-slice_bitcast_fusion.1), channel_id=1, source_target_pairs={{0,8},{4,12},{8,0},{12,4},{16,24},{20,28},{24,16},{28,20},{1,9},{5... | collective-permute-start | bytes 1228808 | tf_op jit(solution)/shard_map/ppermute | solution.py:371
  88.7 12.4 %collective-permute-start.17 = (bf16[2,2,80,640]{3,2,0,1:T(8,128)(2,1)S(1)}, bf16[2,2,80,640]{3,2,0,1:T(8,128)(2,1)S(1)}, u32[]{:S(2)}, u32[]{:S(2)}) collective-permute-start(bf16[2,2,80,640]{3,2,0,1:T(8,128)(2,1)S(1)} %bitcast.116), channel_id=1, source_target_pairs={{0,4},{4,0},{8,12},{12,8},{16,20},{20,16},{24,28},{28,24},{1,5},{5... | collective-permute-start | bytes 1228808 | tf_op jit(solution)/shard_map/ppermute | solution.py:371
  90.3 16.8 %collective-permute-start.20 = (bf16[2,2,80,640]{3,2,0,1:T(8,128)(2,1)S(1)}, bf16[2,2,80,640]{3,2,0,1:T(8,128)(2,1)S(1)}, u32[]{:S(2)}, u32[]{:S(2)}) collective-permute-start(bf16[2,2,80,640]{3,2,0,1:T(8,128)(2,1)S(1)} %bitcast.115), channel_id=1, source_target_pairs={{0,4},{4,0},{8,12},{12,8},{16,20},{20,16},{24,28},{28,24},{1,5},{5... | collective-permute-start | bytes 1228808 | tf_op jit(solution)/shard_map/ppermute | solution.py:371
  94.2 14.0 %collective-permute-start.25 = (bf16[80,640]{1,0:T(8,128)(2,1)S(1)}, bf16[80,640]{1,0:T(8,128)(2,1)S(1)}, u32[]{:S(2)}, u32[]{:S(2)}) collective-permute-start(bf16[80,640]{1,0:T(8,128)(2,1)S(1)} %dynamic-slice_bitcast_fusion.6), channel_id=1, source_target_pairs={{0,4},{4,0},{8,12},{12,8},{16,20},{20,16},{24,28},{28,24},{1,5},{5... | collective-permute-start | bytes 307208 | tf_op jit(solution)/shard_map/ppermute | solution.py:371
  99.0 10.2 %collective-permute-start.15 = (bf16[2,80,640]{2,1,0:T(8,128)(2,1)S(1)}, bf16[2,80,640]{2,1,0:T(8,128)(2,1)S(1)}, u32[]{:S(2)}, u32[]{:S(2)}) collective-permute-start(bf16[2,80,640]{2,1,0:T(8,128)(2,1)S(1)} %dynamic-slice_bitcast_fusion.5), channel_id=1, source_target_pairs={{0,16},{4,20},{8,24},{12,28},{16,0},{20,4},{24,8},{28,12},{1,17},{... | collective-permute-start | bytes 614408 | tf_op jit(solution)/shard_map/ppermute | solution.py:371
  101.3 10.4 %collective-permute-start.18 = (bf16[2,80,640]{2,1,0:T(8,128)(2,1)S(1)}, bf16[2,80,640]{2,1,0:T(8,128)(2,1)S(1)}, u32[]{:S(2)}, u32[]{:S(2)}) collective-permute-start(bf16[2,80,640]{2,1,0:T(8,128)(2,1)S(1)} %dynamic-slice_bitcast_fusion.4), channel_id=1, source_target_pairs={{0,8},{4,12},{8,0},{12,4},{16,24},{20,28},{24,16},{28,20},{1,9},{5... | collective-permute-start | bytes 614408 | tf_op jit(solution)/shard_map/ppermute | solution.py:371
  107.2 7.6 %collective-permute-start.21 = (bf16[2,80,640]{2,1,0:T(8,128)(2,1)S(1)}, bf16[2,80,640]{2,1,0:T(8,128)(2,1)S(1)}, u32[]{:S(2)}, u32[]{:S(2)}) collective-permute-start(bf16[2,80,640]{2,1,0:T(8,128)(2,1)S(1)} %dynamic-slice_bitcast_fusion.3), channel_id=1, source_target_pairs={{0,8},{4,12},{8,0},{12,4},{16,24},{20,28},{24,16},{28,20},{1,9},{5... | collective-permute-start | bytes 614408 | tf_op jit(solution)/shard_map/ppermute | solution.py:371
  108.2 12.4 %collective-permute-start.26 = (f32[80,640]{1,0:T(8,128)S(1)}, f32[80,640]{1,0:T(8,128)S(1)}, u32[]{:S(2)}, u32[]{:S(2)}) collective-permute-start(f32[80,640]{1,0:T(8,128)S(1)} %convert_add_fusion.8), channel_id=1, source_target_pairs={{0,2},{1,3},{2,0},{3,1},{4,6},{5,7},{6,4},{7,5},{8,10},{9,11},{10,... | collective-permute-start | bytes 614408 | tf_op jit(solution)/shard_map/ppermute | solution.py:342
  109.3 7.1 %collective-permute-start.16 = (bf16[80,640]{1,0:T(8,128)(2,1)S(1)}, bf16[80,640]{1,0:T(8,128)(2,1)S(1)}, u32[]{:S(2)}, u32[]{:S(2)}) collective-permute-start(bf16[80,640]{1,0:T(8,128)(2,1)S(1)} %dynamic-slice_bitcast_fusion.9), channel_id=1, source_target_pairs={{0,4},{4,0},{8,12},{12,8},{16,20},{20,16},{24,28},{28,24},{1,5},{5... | collective-permute-start | bytes 307208 | tf_op jit(solution)/shard_map/ppermute | solution.py:371
  111.7 8.2 %collective-permute-start.19 = (bf16[80,640]{1,0:T(8,128)(2,1)S(1)}, bf16[80,640]{1,0:T(8,128)(2,1)S(1)}, u32[]{:S(2)}, u32[]{:S(2)}) collective-permute-start(bf16[80,640]{1,0:T(8,128)(2,1)S(1)} %dynamic-slice_bitcast_fusion.8), channel_id=1, source_target_pairs={{0,16},{4,20},{8,24},{12,28},{16,0},{20,4},{24,8},{28,12},{1,17},{... | collective-permute-start | bytes 307208 | tf_op jit(solution)/shard_map/ppermute | solution.py:371
  114.9 7.2 %collective-permute-start.22 = (bf16[80,640]{1,0:T(8,128)(2,1)S(1)}, bf16[80,640]{1,0:T(8,128)(2,1)S(1)}, u32[]{:S(2)}, u32[]{:S(2)}) collective-permute-start(bf16[80,640]{1,0:T(8,128)(2,1)S(1)} %dynamic-slice_bitcast_fusion.7), channel_id=1, source_target_pairs={{0,16},{4,20},{8,24},{12,28},{16,0},{20,4},{24,8},{28,12},{1,17},{... | collective-permute-start | bytes 307208 | tf_op jit(solution)/shard_map/ppermute | solution.py:371
